TPU v7x, 512 devices: a whole 4x8x8 slice. The times are simulated.
512 devices in a mesh: member: 4 (over x), lat: 16 (over y, core), lon: 8 (over z).
Axes of the slice: x: 4, y: 8, z: 8, core: 2. Of those that a mesh axis runs over, the one named last changes fastest.
Arguments:
- fields: float32 [8, 32, 640, 1024], P('member', None, 'lat', 'lon'), may hold values from -6 to 6
- spectra: float32 [9, 513], replicated, may hold values from 0.3 to 1.5
- band_weights: float32 [9, 640, 5], P(None, 'lat'), may hold values from -2.5 to 2.5
- band_start: int32 [640], P('lat'), may hold values from 0 to 635, as said below
- depth_weights: float32 [32, 9], replicated, may hold values from -2 to 2
- mix_weights: float32 [32, 32], replicated, may hold values from -1 to 1
- target: float32 [32, 640, 1024], P('member', 'lat', 'lon'), may hold values from -6 to 6
Outputs:
- crps: float32 [32, 640, 1024], P('member', 'lat', 'lon')
Inputs may be any that keep to these rules, and one draw needn't show every extreme that they name: For each output row o, band_start[o] lies between o - 5 and o + 5 - 5 + 1; both ends of that offset range occur.
All inputs are finite; a program needn't handle non-finite values.
Results may differ from a plain program's by a relative error of at most 0.0001.
Values sent between devices are 32-bit elements; how exact they have to be, the bound alone decides.
No kernel may reach another device: no remote copies, remote signals or barrier semaphores. Data moves between devices by JAX's collectives and lax.ppermute only.
A program may use at most 64 MiB of HBM per device.

v0:
```python
import functools
import math

import jax
import jax.numpy as jnp
import ml_dtypes
import numpy as np
from jax import lax
from jax.experimental import pallas as pl
from jax.experimental.pallas import tpu as pltpu
from jax.sharding import PartitionSpec as P

PTS = 8
TILE = 128
LENGTH = PTS * TILE
ROWPAD = 64
HALO = 8
S2 = math.sqrt(0.5)


def slot_frequencies():
    f1 = np.arange(TILE)
    zero = np.where(f1 <= 64, 8 * f1, 8 * (f1 - 64))
    four = 8 * (f1 % 64) + 4
    parts = [zero, four]
    for f0 in (1, 2, 3):
        f = 8 * f1 + f0
        f = np.minimum(f, LENGTH - f)
        parts += [f, f]
    return np.concatenate(parts).astype(np.int32)


def slot_scales():
    scale = np.full((LENGTH,), 2.0 / LENGTH)
    scale[0] = 1.0 / LENGTH
    scale[64] = 1.0 / LENGTH
    return scale.astype(np.float32)


def dft_tables():
    r = np.arange(TILE)[:, None]
    f1 = np.arange(TILE)[None, :]

    def ang(f):
        return 2.0 * np.pi * ((r * f) % LENGTH) / LENGTH

    tabs = np.zeros((4, 256, 256))
    low = f1 <= 64
    fz = np.where(low, 8 * f1, 8 * (f1 - 64))
    tabs[0, :TILE, :TILE] = np.where(low, np.cos(ang(fz)), -np.sin(ang(fz)))
    ff = 8 * (f1 % 64) + 4
    tabs[0, TILE:, TILE:] = np.where(f1 < 64, np.cos(ang(ff)), -np.sin(ang(ff)))
    for f0 in (1, 2, 3):
        a = ang(8 * f1 + f0)
        c, s = np.cos(a), np.sin(a)
        tabs[f0, :TILE, :TILE] = c
        tabs[f0, TILE:, :TILE] = s
        tabs[f0, :TILE, TILE:] = -s
        tabs[f0, TILE:, TILE:] = c
    full = tabs.astype(np.float32)
    hi = full.astype(ml_dtypes.bfloat16)
    lo = (tabs - hi.astype(np.float64)).astype(ml_dtypes.bfloat16)
    return hi, lo


def split(x):
    hi = x.astype(jnp.bfloat16)
    lo = (x - hi.astype(jnp.float32)).astype(jnp.bfloat16)
    return hi, lo


def mm(a, b):
    return jnp.dot(a, b, preferred_element_type=jnp.float32)


def mm_t(a, b):
    return lax.dot_general(a, b, (((1,), (1,)), ((), ())), preferred_element_type=jnp.float32)


def dot3(x, t_hi, t_lo, op):
    hi, lo = split(x)
    return op(hi, t_hi) + op(lo, t_hi) + op(hi, t_lo)


def forward_kernel(x_ref, hi_ref, lo_ref, o_ref, top_ref, bot_ref, *, circles, rows):
    x = [x_ref[q] for q in range(PTS)]
    a = [x[q] + x[q + 4] for q in range(4)]
    b = [x[q] - x[q + 4] for q in range(4)]
    e, g = a[0] + a[2], a[1] + a[3]
    p, m = S2 * (b[1] + b[3]), S2 * (b[1] - b[3])
    pairs = [
        (e + g, e - g),
        (b[0] + m, -p - b[2]),
        (a[0] - a[2], a[3] - a[1]),
        (b[0] - m, b[2] - p),
    ]
    for i, pair in enumerate(pairs):
        z = dot3(jnp.concatenate(pair, axis=1), hi_ref[i], lo_ref[i], mm)
        z = z.reshape(circles, rows, 256)
        lanes = slice(256 * i, 256 * (i + 1))
        o_ref[:, :, lanes] = z
        top_ref[:, :, lanes] = z[:, :HALO]
        bot_ref[:, :, lanes] = z[:, rows - HALO :]


def inverse_kernel(x_ref, up_ref, dn_ref, sel_ref, fac_ref, hi_ref, lo_ref, o_ref, y_ref, *, circles, rows, own_vars, n_basis):
    s_hi, s_lo = split(sel_ref[...])
    lhs = jnp.concatenate([s_hi, s_lo, s_hi], axis=1)
    pad = jnp.zeros((ROWPAD - rows - 2 * HALO, 256), jnp.float32)
    v = []
    for i in range(4):
        lanes = slice(256 * i, 256 * (i + 1))
        for c in range(circles):
            ext = jnp.concatenate([x_ref[c, :, lanes], up_ref[c, :, lanes], dn_ref[c, :, lanes], pad], axis=0)
            hi, lo = split(ext)
            z = mm(lhs, jnp.concatenate([hi, hi, lo], axis=0))
            fac = fac_ref[c % own_vars, :, lanes]
            acc = fac[0:1] * z[:rows]
            for k in range(1, n_basis):
                acc = acc + fac[k : k + 1] * z[k * rows : (k + 1) * rows]
            y_ref[c * rows : (c + 1) * rows, :] = acc
        v.append(dot3(y_ref[...], hi_ref[i], lo_ref[i], mm_t))
    v0, v4 = v[0][:, :TILE], v[0][:, TILE:]
    v1r, v1i = v[1][:, :TILE], v[1][:, TILE:]
    v2r, v2i = v[2][:, :TILE], v[2][:, TILE:]
    v3r, v3i = v[3][:, :TILE], v[3][:, TILE:]
    s, d = v0 + v4, v0 - v4
    even = [s + v2r, d - v2i, s - v2r, d + v2i]
    dr, si = v1r - v3r, v1i + v3i
    odd = [v1r + v3r, S2 * (dr - si), v3i - v1i, S2 * (-dr - si)]
    for q in range(4):
        o_ref[q] = even[q] + odd[q]
        o_ref[q + 4] = even[q] - odd[q]


def mix_kernel(x_ref, mix_ref, o_ref, *, n_lon, members, own_vars, rows, group):
    variables = n_lon * own_vars
    m_hi, m_lo = split(mix_ref[...])
    for rb in range(rows // 8):
        part = slice(rb * 8, rb * 8 + 8)
        data = jnp.concatenate(
            [x_ref[:, m, :, part, :].reshape(variables * 8, TILE) for m in range(members)], axis=1
        )
        hi, lo = split(data)
        z = mm(m_hi, hi) + mm(m_hi, lo) + mm(m_lo, hi)
        h = 0.5 * z * (1.0 + lax.erf(z * S2))
        for m in range(members):
            o_ref[:, m, :, part, :] = h[:, m * TILE : (m + 1) * TILE].reshape(
                variables // group, group, 8, TILE
            )


def score_kernel(h_ref, t_ref, o_ref, *, total):
    h = [h_ref[m] for m in range(total)]
    t = t_ref[...]
    skill = jnp.abs(h[0] - t)
    for m in range(1, total):
        skill = skill + jnp.abs(h[m] - t)
    spread = None
    for i in range(total):
        for j in range(i):
            d = jnp.abs(h[i] - h[j])
            spread = d if spread is None else spread + d
    o_ref[...] = skill * (1.0 / total) - spread * (1.0 / (total * total))


def local(fields, spectra, band_weights, band_start, depth_weights, mix_weights, target):
    members, variables, rows, tile = fields.shape
    n_basis = spectra.shape[0]
    band_len = band_weights.shape[2]
    n_member = lax.axis_size("member")
    n_lon = lax.axis_size("lon")
    n_lat = lax.axis_size("lat")
    own_vars = variables // n_lon
    circles = members * own_vars
    group = variables // n_member
    f32 = jnp.float32

    send = fields.reshape(members, n_lon, own_vars, rows, tile).transpose(1, 0, 2, 3, 4)
    recv = lax.all_to_all(send, "lon", split_axis=0, concat_axis=0, tiled=True)

    hi_np, lo_np = dft_tables()
    hi, lo = jnp.asarray(hi_np), jnp.asarray(lo_np)

    local_start = band_start - lax.axis_index("lat") * rows
    read = local_start[:, None] + jnp.arange(band_len, dtype=jnp.int32)[None, :]
    pos = jnp.where(read < 0, rows + HALO + read, jnp.where(read < rows, read, read + HALO))
    cols = jnp.arange(ROWPAD, dtype=jnp.int32)
    sel = jnp.zeros((n_basis, rows, ROWPAD), f32)
    for j in range(band_len):
        sel = sel + jnp.where(pos[None, :, j, None] == cols, band_weights[:, :, j, None], 0.0)
    sel = sel.reshape(n_basis * rows, ROWPAD)

    freq = jnp.asarray(slot_frequencies())
    pick = (jnp.arange(spectra.shape[1], dtype=jnp.int32)[:, None] == freq[None, :]).astype(f32)
    spec = jnp.dot(spectra, pick, precision=lax.Precision.HIGHEST) * slot_scales()[None, :]
    depth = lax.dynamic_slice_in_dim(depth_weights, lax.axis_index("lon") * own_vars, own_vars, 0)
    factor = depth[:, :, None] * spec[None]

    kron = (
        mix_weights[:, None, :, None] * jnp.eye(8, dtype=f32)[None, :, None, :]
    ).reshape(variables * 8, variables * 8)

    flat = circles * rows
    x, top, bot = pl.pallas_call(
        functools.partial(forward_kernel, circles=circles, rows=rows),
        out_shape=(
            jax.ShapeDtypeStruct((circles, rows, LENGTH), f32),
            jax.ShapeDtypeStruct((circles, HALO, LENGTH), f32),
            jax.ShapeDtypeStruct((circles, HALO, LENGTH), f32),
        ),
        name="forward",
    )(recv.reshape(n_lon, flat, tile), hi, lo)

    up = [(i, i + 1) for i in range(n_lat - 1)]
    down = [(i + 1, i) for i in range(n_lat - 1)]
    before = lax.ppermute(bot, "lat", up)
    after = lax.ppermute(top, "lat", down)

    smooth = pl.pallas_call(
        functools.partial(inverse_kernel, circles=circles, rows=rows, own_vars=own_vars, n_basis=n_basis),
        out_shape=jax.ShapeDtypeStruct((n_lon, flat, tile), f32),
        scratch_shapes=[pltpu.VMEM((flat, 256), f32)],
        name="inverse",
    )(x, before, after, sel, factor, hi, lo)

    tiles = lax.all_to_all(
        smooth.reshape(n_lon, members, own_vars, rows, tile), "lon", split_axis=0, concat_axis=0, tiled=True
    )
    hidden = pl.pallas_call(
        functools.partial(
            mix_kernel, n_lon=n_lon, members=members, own_vars=own_vars, rows=rows, group=group
        ),
        out_shape=jax.ShapeDtypeStruct((n_member, members, group, rows, tile), f32),
        name="mix",
    )(tiles, kron)

    every = lax.all_to_all(hidden, "member", split_axis=0, concat_axis=0, tiled=True)
    total = n_member * members
    return pl.pallas_call(
        functools.partial(score_kernel, total=total),
        out_shape=jax.ShapeDtypeStruct(target.shape, f32),
        name="score",
    )(every.reshape(total, group, rows, tile), target)


def solution(mesh):
    in_specs = (
        P("member", None, "lat", "lon"),
        P(),
        P(None, "lat", None),
        P("lat"),
        P(),
        P(),
        P("member", "lat", "lon"),
    )
    out_specs = P("member", "lat", "lon")
    return jax.shard_map(local, mesh=mesh, in_specs=in_specs, out_specs=out_specs, check_vma=False)
```

profile of v0, /device:TPU:16, one launch (start us, length us, event | category | flops | bytes accessed | tf_op | source)
XLA Modules:
  0.0 137.2 jit_solution(10500812144415195607)
XLA Ops:
  0.0 0.0 copy-start
  0.0 2.5 %copy.17 = f32[2,8,4,40,128]{4,3,2,0,1:T(8,128)} copy(f32[2,8,4,40,128]{4,3,2,1,0:T(8,128)} %bitcast.35) | data formatting | bytes 2621440 | tf_op jit(solution)/shard_map/reshape | solution.py:179
  2.5 0.0 copy-start.6
  2.5 0.0 copy-start.8
  2.5 0.0 copy-start.9
  2.5 0.0 copy-start.10
  2.5 10.5 %all-to-all-start = ((f32[8,2,4,40,128]{4,3,2,1,0:T(8,128)}), f32[8,2,4,40,128]{4,3,2,1,0:T(8,128)S(1)}, u32[]{:S(2)}, u32[]{:S(2)}) async-start(f32[8,2,4,40,128]{4,3,2,1,0:T(8,128)} %bitcast.31), calls=%async_computation | async-start | bytes 2621440 | tf_op jit(solution)/shard_map/all_to_all | solution.py:180
  13.0 0.0 copy-done.6
  13.0 0.1 slice_reduce_fusion.4
  13.1 0.0 copy-done.8
  13.1 0.1 iota_compare_fusion.10
  13.2 0.1 iota_compare_fusion.6
  13.3 0.1 iota_compare_fusion.8
  13.3 0.0 copy-done
  13.4 0.0 copy-done.9
  13.4 0.0 copy-done.10
  13.4 0.8 fusion.2
  14.2 0.0 copy-start.7
  14.2 33.2 %all-to-all-done = f32[8,2,4,40,128]{4,3,2,1,0:T(8,128)S(1)} async-done(((f32[8,2,4,40,128]{4,3,2,1,0:T(8,128)}), f32[8,2,4,40,128]{4,3,2,1,0:T(8,128)S(1)}, u32[]{:S(2)}, u32[]{:S(2)}) %all-to-all-start) | async-done | bytes 1310752 | tf_op jit(solution)/shard_map/all_to_all | solution.py:180
  47.4 0.0 copy-start.1
  47.4 1.1 copy-done.1
  48.5 3.6 %forward.1 = (f32[8,40,1024]{2,1,0:T(8,128)}, f32[8,8,1024]{2,1,0:T(8,128)}, f32[8,8,1024]{2,1,0:T(8,128)}) custom-call(f32[8,320,128]{2,1,0:T(8,128)} %bitcast.32, bf16[4,256,256]{2,1,0:T(8,128)(2,1)} %constant.33.clone.hi_ref, bf16[4,256,256]{2,1,0:T(8,128)(2,1)} %constant.34.clone.lo_ref), custom_call_target="tpu_custom_call" | custom-call | tf_op jit(solution)/shard_map/forward/pallas_call | solution.py:205
  52.0 1.9 %collective-permute-start = (f32[8,8,1024]{2,1,0:T(8,128)}, f32[8,8,1024]{2,1,0:T(8,128)S(1)}, u32[]{:S(2)}, u32[]{:S(2)}) collective-permute-start(f32[8,8,1024]{2,1,0:T(8,128)} %get-tuple-element.9), channel_id=1, source_target_pairs={{0,8},{8,16},{16,24},{24,32},{32,40},{40,48},{48,56},{56,64},{64,7... | collective-permute-start | bytes 786440 | tf_op jit(solution)/shard_map/ppermute | solution.py:217
  54.0 3.6 %collective-permute-start.1 = (f32[8,8,1024]{2,1,0:T(8,128)}, f32[8,8,1024]{2,1,0:T(8,128)S(1)}, u32[]{:S(2)}, u32[]{:S(2)}) collective-permute-start(f32[8,8,1024]{2,1,0:T(8,128)} %get-tuple-element.10), channel_id=1, source_target_pairs={{8,0},{16,8},{24,16},{32,24},{40,32},{48,40},{56,48},{64,56},{72,6... | collective-permute-start | bytes 786440 | tf_op jit(solution)/shard_map/ppermute | solution.py:218
  57.6 0.0 copy-done.7
  57.6 0.1 constant_dynamic-slice_fusion
  57.7 0.1 copy.15
  57.8 0.1 broadcast_in_dim.99
  57.9 0.1 broadcast_in_dim.108
  58.0 0.1 broadcast_in_dim.104
  58.0 0.1 broadcast_in_dim.116
  58.1 0.1 broadcast_in_dim.112
  58.2 1.0 select_add_fusion.sel_ref
  59.2 0.8 broadcast_multiply_fusion.1.fac_ref
  60.0 0.0 collective-permute-done.up_ref
  60.0 0.0 copy-start.3
  60.0 1.8 %collective-permute-done.1.dn_ref = f32[8,8,1024]{2,1,0:T(8,128)S(1)} collective-permute-done((f32[8,8,1024]{2,1,0:T(8,128)}, f32[8,8,1024]{2,1,0:T(8,128)S(1)}, u32[]{:S(2)}, u32[]{:S(2)}) %collective-permute-start.1) | collective-permute-done | bytes 262176 | tf_op jit(solution)/shard_map/ppermute | solution.py:218
  61.8 0.0 copy-start.4
  61.8 0.0 copy-done.3
  61.8 0.7 copy-done.4
  62.5 5.8 %inverse.1 = f32[8,320,128]{2,1,0:T(8,128)} custom-call(f32[8,40,1024]{2,1,0:T(8,128)} %get-tuple-element.8.x_ref, f32[8,8,1024]{2,1,0:T(8,128)} %copy-done.3, f32[8,8,1024]{2,1,0:T(8,128)} %copy-done.4, f32[360,64]{1,0:T(8,128)} %select_add_fusion.sel_ref, f32[4,9,1024]{2,1,0:T(8,128)} %broadcast_multiply_fusion.1.fac_ref, ...), custom_call_target="tpu_custom_call" | custom-call | tf_op jit(solution)/shard_map/inverse/pallas_call | solution.py:220
  68.3 0.0 copy-start.5
  68.3 3.7 %all-to-all-start.1 = ((f32[8,2,4,40,128]{4,3,2,1,0:T(8,128)}), f32[8,2,4,40,128]{4,3,2,1,0:T(8,128)S(1)}, u32[]{:S(2)}, u32[]{:S(2)}) async-start(f32[8,2,4,40,128]{4,3,2,1,0:T(8,128)} %bitcast.34), calls=%async_computation.1 | async-start | bytes 2621440 | tf_op jit(solution)/shard_map/all_to_all | solution.py:227
  72.0 0.0 copy-done.5
  72.0 2.5 %broadcast_multiply_fusion = f32[32,8,32,8]{3,2,1,0:T(8,128)} fusion(f32[8,8]{1,0:T(8,128)S(1)} %fusion.6, f32[32,32]{1,0:T(8,128)S(1)} %copy-done.5), kind=kLoop, calls=%fused_computation.2 | loop fusion | flops 65536 | bytes 266496 | tf_op jit(solution)/shard_map/mul | solution.py:201
  74.5 4.7 %mul.61.mix_ref = f32[256,256]{1,0:T(8,128)} reshape(f32[32,8,32,8]{3,2,1,0:T(8,128)} %broadcast_multiply_fusion) | data formatting | bytes 524288 | tf_op jit(solution)/shard_map/mul | solution.py:201
  79.2 28.4 %all-to-all-done.1.x_ref = f32[8,2,4,40,128]{4,3,2,1,0:T(8,128)S(1)} async-done(((f32[8,2,4,40,128]{4,3,2,1,0:T(8,128)}), f32[8,2,4,40,128]{4,3,2,1,0:T(8,128)S(1)}, u32[]{:S(2)}, u32[]{:S(2)}) %all-to-all-start.1) | async-done | bytes 1310752 | tf_op jit(solution)/shard_map/all_to_all | solution.py:227
  107.6 0.0 copy-start.2
  107.6 1.1 copy-done.2
  108.7 3.1 %mix.1 = f32[4,2,8,40,128]{4,3,2,1,0:T(8,128)} custom-call(f32[8,2,4,40,128]{4,3,2,1,0:T(8,128)} %copy-done.2, f32[256,256]{1,0:T(8,128)} %mul.61.mix_ref), custom_call_target="tpu_custom_call" | custom-call | tf_op jit(solution)/shard_map/mix/pallas_call | solution.py:230
  111.8 22.8 %all_to_all.15 = f32[4,2,8,40,128]{4,3,2,1,0:T(8,128)} all-to-all(f32[4,2,8,40,128]{4,3,2,1,0:T(8,128)} %mix.1), channel_id=1, replica_groups=mesh['member'=4,'lat'=16,'lon'=8] {'member'}, dimensions={0} | all-to-all | bytes 2621440 | tf_op jit(solution)/shard_map/all_to_all | solution.py:238
  134.7 2.6 %score.1 = f32[8,40,128]{2,1,0:T(8,128)} custom-call(f32[8,8,40,128]{3,2,1,0:T(8,128)} %bitcast.33, f32[8,40,128]{2,1,0:T(8,128)} %t_ref.1), custom_call_target="tpu_custom_call" | custom-call | tf_op jit(solution)/shard_map/score/pallas_call | solution.py:240
  (4 shorter events, 0.0 us)
Async XLA Ops:
  0.0 13.3 %copy-start = (f32[9,513]{1,0:T(8,128)S(1)}, f32[9,513]{1,0:T(8,128)}, u32[]{:S(2)}) copy-start(f32[9,513]{1,0:T(8,128)} %param.12) | copy-start | bytes 55408
  2.5 10.5 %copy-start.6 = (f32[9,40,5]{1,2,0:T(8,128)S(1)}, f32[9,40,5]{1,2,0:T(8,128)}, u32[]{:S(2)}) copy-start(f32[9,40,5]{1,2,0:T(8,128)} %param.13) | copy-start | bytes 21604
  2.5 10.6 %copy-start.8 = (s32[40]{0:T(128)S(1)}, s32[40]{0:T(128)}, u32[]{:S(2)}) copy-start(s32[40]{0:T(128)} %param.14) | copy-start | bytes 484
  2.5 10.9 %copy-start.9 = (f32[1024]{0:T(1024)S(1)}, f32[1024]{0:T(1024)}, u32[]{:S(2)}) copy-start(f32[1024]{0:T(1024)} %constant.41) | copy-start | bytes 12292
  2.5 10.9 %copy-start.10 = (s32[1024]{0:T(1024)S(1)}, s32[1024]{0:T(1024)}, u32[]{:S(2)}) copy-start(s32[1024]{0:T(1024)} %constant.35.clone) | copy-start | bytes 12292
  2.5 44.9 %all-to-all-start = ((f32[8,2,4,40,128]{4,3,2,1,0:T(8,128)}), f32[8,2,4,40,128]{4,3,2,1,0:T(8,128)S(1)}, u32[]{:S(2)}, u32[]{:S(2)}) async-start(f32[8,2,4,40,128]{4,3,2,1,0:T(8,128)} %bitcast.31), calls=%async_computation | async-start | bytes 2621440 | tf_op jit(solution)/shard_map/all_to_all | solution.py:180
  14.2 43.4 %copy-start.7 = (f32[32,9]{0,1:T(8,128)S(1)}, f32[32,9]{0,1:T(8,128)}, u32[]{:S(2)}) copy-start(f32[32,9]{0,1:T(8,128)} %param.15) | copy-start | bytes 3460
  47.4 1.1 copy-start.1
  52.0 7.9 %collective-permute-start = (f32[8,8,1024]{2,1,0:T(8,128)}, f32[8,8,1024]{2,1,0:T(8,128)S(1)}, u32[]{:S(2)}, u32[]{:S(2)}) collective-permute-start(f32[8,8,1024]{2,1,0:T(8,128)} %get-tuple-element.9), channel_id=1, source_target_pairs={{0,8},{8,16},{16,24},{24,32},{32,40},{40,48},{48,56},{56,64},{64,7... | collective-permute-start | bytes 786440 | tf_op jit(solution)/shard_map/ppermute | solution.py:217
  54.0 7.8 %collective-permute-start.1 = (f32[8,8,1024]{2,1,0:T(8,128)}, f32[8,8,1024]{2,1,0:T(8,128)S(1)}, u32[]{:S(2)}, u32[]{:S(2)}) collective-permute-start(f32[8,8,1024]{2,1,0:T(8,128)} %get-tuple-element.10), channel_id=1, source_target_pairs={{8,0},{16,8},{24,16},{32,24},{40,32},{48,40},{56,48},{64,56},{72,6... | collective-permute-start | bytes 786440 | tf_op jit(solution)/shard_map/ppermute | solution.py:218
  60.0 1.8 %copy-start.3 = (f32[8,8,1024]{2,1,0:T(8,128)}, f32[8,8,1024]{2,1,0:T(8,128)S(1)}, u32[]{:S(2)}) copy-start(f32[8,8,1024]{2,1,0:T(8,128)S(1)} %collective-permute-done.up_ref) | copy-start | bytes 786436
  61.8 0.7 copy-start.4
  68.3 3.7 %copy-start.5 = (f32[32,32]{1,0:T(8,128)S(1)}, f32[32,32]{1,0:T(8,128)}, u32[]{:S(2)}) copy-start(f32[32,32]{1,0:T(8,128)} %param.16) | copy-start | bytes 12292
  68.3 39.4 %all-to-all-start.1 = ((f32[8,2,4,40,128]{4,3,2,1,0:T(8,128)}), f32[8,2,4,40,128]{4,3,2,1,0:T(8,128)S(1)}, u32[]{:S(2)}, u32[]{:S(2)}) async-start(f32[8,2,4,40,128]{4,3,2,1,0:T(8,128)} %bitcast.34), calls=%async_computation.1 | async-start | bytes 2621440 | tf_op jit(solution)/shard_map/all_to_all | solution.py:227
  107.6 1.1 copy-start.2
where the time goes:
time: 138 us; the launch traced here: 137 us
  waiting for transfers between devices  63.4 us (46%)
  blocking collectives  22.8 us (17%)
  starting transfers between devices  19.7 us (14%)
  Pallas kernels  15 us (11%)
  local copies, waits for them, and re-layouts  10.7 us (8%)
  other arithmetic  4.55 us (3%)
    all_to_all x1, waiting for transfers between devices, local(): recv = lax.all_to_all(send, 'lon', split_axis=0, concat_axis=0, tiled=True)  33.2 us
    all_to_all x1, waiting for transfers between devices, local(): lax.all_to_all(smooth.reshape(n_lon, members, own_vars, rows, tile), 'lon...  28.4 us
    all_to_all x1, blocking collectives, local(): lax.all_to_all(hidden, 'member', split_axis=0, concat_axis=0, tiled=True)  22.8 us
    all_to_all x1, starting transfers between devices, local(): recv = lax.all_to_all(send, 'lon', split_axis=0, concat_axis=0, tiled=True)  10.5 us
    pallas_call x1, Pallas kernels, local(): pl.pallas_call(functools.partial(inverse_kernel, circles=circles, rows=ro...  5.78 us
    mul x1, local copies, waits for them, and re-layouts, local(): mix_weights[:, None, :, None] * jnp.eye(8, dtype=f32)[None, :, None, :]  4.68 us
    all_to_all x1, starting transfers between devices, local(): lax.all_to_all(smooth.reshape(n_lon, members, own_vars, rows, tile), 'lon...  3.7 us
    ppermute x1, starting transfers between devices, local(): after = lax.ppermute(top, 'lat', down)  3.64 us
  transfers between devices with their start and end apart: 4, of which 3 were waited for; matrix products, arithmetic and copies ran while one was open for 8% of the time, Pallas kernels for 0%

commit v1 on v0

v1 whole, which is shorter than its diff:
```python
import functools
import math

import jax
import jax.numpy as jnp
import ml_dtypes
import numpy as np
from jax import lax
from jax.experimental import pallas as pl
from jax.experimental.pallas import tpu as pltpu
from jax.sharding import PartitionSpec as P


PTS = 8
TILE = 128
LENGTH = PTS * TILE
ROWPAD = 64
HALO = 8
S2 = math.sqrt(0.5)


def slot_frequencies():
    f1 = np.arange(TILE)
    zero = np.where(f1 <= 64, 8 * f1, 8 * (f1 - 64))
    four = 8 * (f1 % 64) + 4
    parts = [zero, four]
    for f0 in (1, 2, 3):
        f = 8 * f1 + f0
        f = np.minimum(f, LENGTH - f)
        parts += [f, f]
    return np.concatenate(parts).astype(np.int32)


def slot_scales():
    scale = np.full((LENGTH,), 2.0 / LENGTH)
    scale[0] = 1.0 / LENGTH
    scale[64] = 1.0 / LENGTH
    return scale.astype(np.float32)


def dft_tables():
    r = np.arange(TILE)[:, None]
    f1 = np.arange(TILE)[None, :]

    def ang(f):
        return 2.0 * np.pi * ((r * f) % LENGTH) / LENGTH

    tabs = np.zeros((4, 256, 256))
    low = f1 <= 64
    fz = np.where(low, 8 * f1, 8 * (f1 - 64))
    tabs[0, :TILE, :TILE] = np.where(low, np.cos(ang(fz)), -np.sin(ang(fz)))
    ff = 8 * (f1 % 64) + 4
    tabs[0, TILE:, TILE:] = np.where(f1 < 64, np.cos(ang(ff)), -np.sin(ang(ff)))
    for f0 in (1, 2, 3):
        a = ang(8 * f1 + f0)
        c, s = np.cos(a), np.sin(a)
        tabs[f0, :TILE, :TILE] = c
        tabs[f0, TILE:, :TILE] = s
        tabs[f0, :TILE, TILE:] = -s
        tabs[f0, TILE:, TILE:] = c
    full = tabs.astype(np.float32)
    hi = full.astype(ml_dtypes.bfloat16)
    lo = (tabs - hi.astype(np.float64)).astype(ml_dtypes.bfloat16)
    return hi, lo


def split(x):
    hi = x.astype(jnp.bfloat16)
    lo = (x - hi.astype(jnp.float32)).astype(jnp.bfloat16)
    return hi, lo


def mm(a, b):
    return jnp.dot(a, b, preferred_element_type=jnp.float32)


def mm_t(a, b):
    return lax.dot_general(a, b, (((1,), (1,)), ((), ())), preferred_element_type=jnp.float32)


def dot3(x, t_hi, t_lo, op):
    hi, lo = split(x)
    return op(hi, t_hi) + op(lo, t_hi) + op(hi, t_lo)


def analyse(x, hi_ref, lo_ref, store):
    a = [x[q] + x[q + 4] for q in range(4)]
    b = [x[q] - x[q + 4] for q in range(4)]
    e, g = a[0] + a[2], a[1] + a[3]
    p, m = S2 * (b[1] + b[3]), S2 * (b[1] - b[3])
    pairs = [
        (e + g, e - g),
        (b[0] + m, -p - b[2]),
        (a[0] - a[2], a[3] - a[1]),
        (b[0] - m, b[2] - p),
    ]
    for i, pair in enumerate(pairs):
        store(i, dot3(jnp.concatenate(pair, axis=1), hi_ref[i], lo_ref[i], mm))


def forward_kernel(x_ref, hi_ref, lo_ref, top_ref, mid_ref, bot_ref, *, circles, rows):
    def store(i, z):
        lanes = slice(256 * i, 256 * (i + 1))
        z = z.reshape(circles, rows, 256)
        top_ref[:, :, lanes] = z[:, :HALO]
        mid_ref[:, :, lanes] = z[:, HALO : rows - HALO]
        bot_ref[:, :, lanes] = z[:, rows - HALO :]

    analyse([x_ref[q] for q in range(PTS)], hi_ref, lo_ref, store)


def banded(ext, lhs, fac, count, n_basis):
    hi, lo = split(ext)
    z = mm(lhs, jnp.concatenate([hi, hi, lo], axis=0))
    acc = fac[0:1] * z[:count]
    for k in range(1, n_basis):
        acc = acc + fac[k : k + 1] * z[k * count : (k + 1) * count]
    return acc


def wide_selector(sel_ref):
    s_hi, s_lo = split(sel_ref[...])
    return jnp.concatenate([s_hi, s_lo, s_hi], axis=1)


def combine(v):
    v0, v4 = v[0][:, :TILE], v[0][:, TILE:]
    v1r, v1i = v[1][:, :TILE], v[1][:, TILE:]
    v2r, v2i = v[2][:, :TILE], v[2][:, TILE:]
    v3r, v3i = v[3][:, :TILE], v[3][:, TILE:]
    s, d = v0 + v4, v0 - v4
    even = [s + v2r, d - v2i, s - v2r, d + v2i]
    dr, si = v1r - v3r, v1i + v3i
    odd = [v1r + v3r, S2 * (dr - si), v3i - v1i, S2 * (-dr - si)]
    return [e + o for e, o in zip(even, odd)] + [e - o for e, o in zip(even, odd)]


def inner_kernel(
    top_ref, mid_ref, bot_ref, sel_ref, fac_ref, hi_ref, lo_ref, o_ref, near_ref, y_ref, *, own_vars, n_basis, parts
):
    circles, count, _ = mid_ref.shape
    near_ref[:, :HALO] = mid_ref[:, :HALO]
    near_ref[:, HALO:] = mid_ref[:, count - HALO :]
    lhs = wide_selector(sel_ref)
    span = 8 * circles
    pad = jnp.zeros((8, 256), jnp.float32)
    v = []
    for i in range(4):
        lanes = slice(256 * i, 256 * (i + 1))
        for mc in range(circles):
            ext = jnp.concatenate([top_ref[mc, :, lanes], mid_ref[mc, :, lanes], bot_ref[mc, :, lanes], pad], axis=0)
            acc = banded(ext, lhs, fac_ref[mc % own_vars, :, lanes], count, n_basis)
            for p in range(parts - 1):
                y_ref[p * span + 8 * mc : p * span + 8 * mc + 8, :] = acc[8 * p : 8 * p + 8]
        v.append(dot3(y_ref[...], hi_ref[i], lo_ref[i], mm_t))
    for q, piece in enumerate(combine(v)):
        for p in range(parts - 1):
            o_ref[p, q] = piece[p * span : (p + 1) * span]


def edge_kernel(
    top_ref, bot_ref, near_ref, up_ref, dn_ref, in_ref, sel_ref, fac_ref, hi_ref, lo_ref, o_ref, y_ref, *, members, own_vars, n_basis, parts, tail
):
    lhs = wide_selector(sel_ref)
    span = 8 * members * own_vars
    main, rest = 8 * own_vars, tail * own_vars
    v = []
    for i in range(4):
        lanes = slice(256 * i, 256 * (i + 1))
        for m in range(members):
            for c in range(own_vars):
                mc = m * own_vars + c
                ext = jnp.concatenate(
                    [ref[mc, :, lanes] for ref in (top_ref, near_ref, bot_ref, up_ref, dn_ref)], axis=0
                )
                acc = banded(ext, lhs, fac_ref[c, :, lanes], 16, n_basis)
                y_ref[8 * mc : 8 * mc + 8, :] = acc[:8]
                for p in range(parts):
                    lead = span + (p * members + m) * rest + tail * c
                    y_ref[lead : lead + tail, :] = acc[8 + tail * p : 8 + tail * (p + 1)]
        v.append(dot3(y_ref[...], hi_ref[i], lo_ref[i], mm_t))
    for q, piece in enumerate(combine(v)):
        for p in range(parts):
            for m in range(members):
                at = m * (main + rest)
                if p:
                    o_ref[p, q, at : at + main] = in_ref[p - 1, q, m * main : (m + 1) * main]
                else:
                    o_ref[p, q, at : at + main] = piece[m * main : (m + 1) * main]
                lead = span + (p * members + m) * rest
                o_ref[p, q, at + main : at + main + rest] = piece[lead : lead + rest]


def send_kernel(x_ref, o_ref, buf_ref, in_sem, out_sem, *, members, n_lon, own_vars):
    loads, stores = [], []
    for z in range(n_lon):
        for m in range(members):
            loads.append(
                pltpu.make_async_copy(
                    x_ref.at[m, pl.ds(z * own_vars, own_vars)],
                    buf_ref.at[z, pl.ds(m * own_vars, own_vars)],
                    in_sem.at[z * members + m],
                )
            )
        stores.append(pltpu.make_async_copy(buf_ref.at[z], o_ref.at[z], out_sem.at[z]))
    for copy in loads:
        copy.start()
    for z in range(n_lon):
        for m in range(members):
            loads[z * members + m].wait()
        stores[z].start()
    for copy in stores:
        copy.wait()


def mixed(x_ref, k_refs, members, own_vars, n_member, n_lon):
    block = x_ref.shape[2] // members
    main = 8 * own_vars
    k_hi, k_lo, r_hi, r_lo = [ref[...] for ref in k_refs]
    out = []
    for m in range(members):
        lead = m * block
        for j in range(0, n_member, 2):
            pair = range(j, min(j + 2, n_member))
            big = jnp.concatenate([x_ref[i, :, lead : lead + main, :].reshape(n_lon * main, TILE) for i in pair], axis=1)
            small = jnp.concatenate(
                [x_ref[i, :, lead + main : lead + block, :].reshape(n_lon * (block - main), TILE) for i in pair], axis=1
            )
            hi, lo = split(big)
            z = mm(k_hi, hi) + mm(k_hi, lo) + mm(k_lo, hi)
            hi, lo = split(small)
            y = mm(r_hi, hi) + mm(r_hi, lo) + mm(r_lo, hi)
            h = jnp.concatenate([z, y], axis=0)
            h = 0.5 * h * (1.0 + lax.erf(h * S2))
            for i in range(len(pair)):
                out.append(h[:, i * TILE : (i + 1) * TILE])
    return out


def score_kernel(*refs, total, main, parts, earlier, sizes):
    prior = refs[:earlier]
    x_ref, *k_refs, t_ref, o_ref, h_ref = refs[earlier:]
    ready = [(ref, i) for ref in prior for i in range(ref.shape[0])]
    for i, h in enumerate(mixed(x_ref, k_refs, **sizes)):
        h_ref[i] = h
        ready.append((h_ref, i))
    width = main // parts
    rest = t_ref.shape[1] - width
    for p in range(parts):
        for lo, n, at in ((p * width, width, 0), (main + p * rest, rest, width)):
            t = t_ref[p, at : at + n, :]
            h = [ref[i, lo : lo + n, :] for ref, i in ready]
            skill = jnp.abs(h[0] - t)
            for m in range(1, total):
                skill = skill + jnp.abs(h[m] - t)
            spread = None
            for i in range(total):
                for j in range(i):
                    d = jnp.abs(h[i] - h[j])
                    spread = d if spread is None else spread + d
            o_ref[p, at : at + n, :] = skill * (1.0 / total) - spread * (1.0 / (total * total))


def spread_rows(t_ref, o_ref, parts, tail):
    group = t_ref.shape[0]
    for p in range(parts):
        for d in range(group):
            o_ref[p, 8 * d : 8 * d + 8, :] = t_ref[d, 8 * p : 8 * p + 8, :]
            lead = 8 * group + tail * d
            row = 8 * parts + tail * p
            o_ref[p, lead : lead + tail, :] = t_ref[d, row : row + tail, :]


def join_rows_kernel(x_ref, o_ref, *, parts, tail):
    group = o_ref.shape[0]
    for p in range(parts):
        for d in range(group):
            o_ref[d, 8 * p : 8 * p + 8, :] = x_ref[p, 8 * d : 8 * d + 8, :]
            lead = 8 * group + tail * d
            row = 8 * parts + tail * p
            o_ref[d, row : row + tail, :] = x_ref[p, lead : lead + tail, :]


def expand(mix, n):
    size = mix.shape[0]
    span = size * n
    rep = lax.broadcasted_iota(jnp.int32, (span, size), 0) // n == lax.broadcasted_iota(jnp.int32, (span, size), 1)
    rep = rep.astype(jnp.float32).astype(jnp.bfloat16)
    row = lax.broadcasted_iota(jnp.int32, (span, span), 0) % n
    col = lax.broadcasted_iota(jnp.int32, (span, span), 1) % n
    full = []
    for part in split(mix):
        tall = mm(rep, part).astype(jnp.bfloat16)
        full.append(jnp.where(row == col, mm_t(tall, rep), 0.0).astype(jnp.bfloat16))
    return full


def prepare_kernel(mix_ref, t_ref, khi_ref, klo_ref, rhi_ref, rlo_ref, o_ref, *, parts, tail):
    khi_ref[...], klo_ref[...] = expand(mix_ref[...], 8)
    rhi_ref[...], rlo_ref[...] = expand(mix_ref[...], tail)
    spread_rows(t_ref, o_ref, parts, tail)


def in_vmem(*arrays):
    return [pltpu.with_memory_space_constraint(a, pltpu.VMEM) for a in arrays]


def block(fields, spectra, band_weights, band_start, depth_weights, mix_weights, target):
    members, variables, rows, tile = fields.shape
    n_basis = spectra.shape[0]
    band_len = band_weights.shape[2]
    n_member = lax.axis_size("member")
    n_lon = lax.axis_size("lon")
    n_lat = lax.axis_size("lat")
    own_vars = variables // n_lon
    group = variables // n_member
    parts = n_member
    tail = (rows - 8 * parts) // parts
    circles = members * own_vars
    f32 = jnp.float32
    vmem = pl.BlockSpec(memory_space=pltpu.VMEM)
    shape = jax.ShapeDtypeStruct

    hbm = pl.BlockSpec(memory_space=pl.ANY)
    send = pl.pallas_call(
        functools.partial(send_kernel, members=members, n_lon=n_lon, own_vars=own_vars),
        out_shape=shape((n_lon, circles, rows, tile), f32),
        in_specs=[hbm],
        out_specs=hbm,
        scratch_shapes=[
            pltpu.VMEM((n_lon, circles, rows, tile), f32),
            pltpu.SemaphoreType.DMA((members * n_lon,)),
            pltpu.SemaphoreType.DMA((n_lon,)),
        ],
        name="send",
    )(fields)
    received = lax.all_to_all(send, "lon", split_axis=0, concat_axis=0, tiled=True)

    width = group * (8 + tail)
    *krons, mine = pl.pallas_call(
        functools.partial(prepare_kernel, parts=parts, tail=tail),
        out_shape=(
            shape((variables * 8, variables * 8), jnp.bfloat16),
            shape((variables * 8, variables * 8), jnp.bfloat16),
            shape((variables * tail, variables * tail), jnp.bfloat16),
            shape((variables * tail, variables * tail), jnp.bfloat16),
            shape((parts, width, tile), f32),
        ),
        name="prepare",
    )(mix_weights, target)
    x_at = lax.axis_index("member")
    wanted = jnp.zeros((parts, width, tile), f32)
    own = lax.dynamic_index_in_dim(mine, x_at, 0, keepdims=True)
    wanted = lax.dynamic_update_slice_in_dim(wanted, own, x_at, 0)
    for s in range(1, n_member):
        ring = [(i, (i + s) % n_member) for i in range(n_member)]
        out = lax.dynamic_index_in_dim(mine, (x_at + s) % n_member, 0, keepdims=True)
        got = lax.ppermute(out, "member", ring)
        wanted = lax.dynamic_update_slice_in_dim(wanted, got, (x_at - s) % n_member, 0)

    hi_np, lo_np = dft_tables()
    hi, lo = jnp.asarray(hi_np), jnp.asarray(lo_np)

    local_start = band_start - lax.axis_index("lat") * rows
    read = local_start[:, None] + jnp.arange(band_len, dtype=jnp.int32)[None, :]
    pos = jnp.where(read < 0, rows + HALO + read, jnp.where(read < rows, read, read + HALO))
    cols = jnp.arange(ROWPAD, dtype=jnp.int32)
    sel = jnp.zeros((n_basis, rows, ROWPAD), f32)
    for j in range(band_len):
        sel = sel + jnp.where(pos[None, :, j, None] == cols, band_weights[:, :, j, None], 0.0)
    inner_sel = sel[:, 8 : rows - 8, : rows + 8].reshape(n_basis * (rows - 16), rows + 8)
    edge_sel = jnp.concatenate([sel[:, :8], sel[:, rows - 8 :]], axis=1)
    edge_sel = jnp.concatenate([edge_sel[:, :, :16], edge_sel[:, :, rows - 16 : rows + 16]], axis=2)
    edge_sel = edge_sel.reshape(n_basis * 16, 48)

    freq = jnp.asarray(slot_frequencies())
    pick = (jnp.arange(spectra.shape[1], dtype=jnp.int32)[:, None] == freq[None, :]).astype(f32)
    spec = jnp.dot(spectra, pick, precision=lax.Precision.HIGHEST) * slot_scales()[None, :]
    depth = lax.dynamic_slice_in_dim(depth_weights, lax.axis_index("lon") * own_vars, own_vars, 0)
    factor = depth[:, :, None] * spec[None]
    received, krons, wanted, inner_sel, edge_sel, factor = lax.optimization_barrier(
        (received, krons, wanted, inner_sel, edge_sel, factor)
    )

    up = [(i, i + 1) for i in range(n_lat - 1)]
    down = [(i + 1, i) for i in range(n_lat - 1)]
    top, mid, bot = pl.pallas_call(
        functools.partial(forward_kernel, circles=circles, rows=rows),
        out_shape=(
            shape((circles, HALO, LENGTH), f32),
            shape((circles, rows - 2 * HALO, LENGTH), f32),
            shape((circles, HALO, LENGTH), f32),
        ),
        in_specs=[vmem] * 3,
        name="forward",
    )(*in_vmem(received.reshape(n_lon, circles * rows, tile)), hi, lo)
    before = lax.ppermute(bot, "lat", up)
    after = lax.ppermute(top, "lat", down)
    inner, near = pl.pallas_call(
        functools.partial(inner_kernel, own_vars=own_vars, n_basis=n_basis, parts=parts),
        out_shape=(
            pltpu.VMEM((parts - 1, n_lon, 8 * circles, tile), f32),
            pltpu.VMEM((circles, 2 * HALO, LENGTH), f32),
        ),
        in_specs=[vmem] * 7,
        out_specs=(vmem, vmem),
        scratch_shapes=[pltpu.VMEM((8 * (parts - 1) * circles, 256), f32)],
        name="inner",
    )(top, mid, bot, inner_sel, factor, hi, lo)
    smooth = pl.pallas_call(
        functools.partial(
            edge_kernel, members=members, own_vars=own_vars, n_basis=n_basis, parts=parts, tail=tail
        ),
        out_shape=shape((parts, n_lon, circles * (8 + tail), tile), f32),
        in_specs=[vmem] * 10,
        scratch_shapes=[pltpu.VMEM((circles * (8 + parts * tail), 256), f32)],
        name="edge",
    )(top, bot, *in_vmem(near, before, after, inner), edge_sel, factor, hi, lo)
    moved = lax.all_to_all(
        smooth.reshape(parts * n_lon, *smooth.shape[2:]),
        ("member", "lon"),
        split_axis=0,
        concat_axis=0,
        tiled=True,
    ).reshape(smooth.shape)

    sizes = dict(members=members, own_vars=own_vars, n_member=n_member, n_lon=n_lon)
    height = variables * (8 + tail)
    total = n_member * members
    scored = pl.pallas_call(
        functools.partial(
            score_kernel, total=total, main=variables * 8, parts=parts, earlier=0, sizes=sizes
        ),
        out_shape=shape((parts, width, tile), f32),
        in_specs=[vmem] * 6,
        scratch_shapes=[pltpu.VMEM((total, height, tile), f32)],
        name="score",
    )(*in_vmem(moved), *krons, *in_vmem(wanted))
    back = lax.all_to_all(scored, "member", split_axis=0, concat_axis=0, tiled=True)
    return pl.pallas_call(
        functools.partial(join_rows_kernel, parts=parts, tail=tail),
        out_shape=shape(target.shape, f32),
        in_specs=[vmem],
        name="join_rows",
    )(*in_vmem(back))


def solution(mesh):
    in_specs = (
        P("member", None, "lat", "lon"),
        P(),
        P(None, "lat", None),
        P("lat"),
        P(),
        P(),
        P("member", "lat", "lon"),
    )
    out_specs = P("member", "lat", "lon")
    return jax.shard_map(block, mesh=mesh, in_specs=in_specs, out_specs=out_specs, check_vma=False)
```

time: 138 us -> 130 us (0.942)
  the two profiles are of different devices: /device:TPU:16 before, /device:TPU:88 now
where the time goes in v1:
time: 130 us; the launch traced here: 129 us
  blocking collectives  50.7 us (39%)
  waiting for transfers between devices  29.7 us (23%)
  starting transfers between devices  24.6 us (19%)
  Pallas kernels  19.2 us (15%)
  other arithmetic  2.05 us (2%)
  local copies, waits for them, and re-layouts  1.8 us (1%)
    all_to_all x1, blocking collectives, block(): lax.all_to_all(smooth.reshape(parts * n_lon, *smooth.shape[2:]), ('member...  41.3 us
    all_to_all x1, waiting for transfers between devices, block(): lax.all_to_all(send, 'lon', split_axis=0, concat_axis=0, tiled=True)  28.1 us
    ppermute x3, starting transfers between devices, block(): got = lax.ppermute(out, 'member', ring)  10.2 us
    all_to_all x1, starting transfers between devices, block(): lax.all_to_all(send, 'lon', split_axis=0, concat_axis=0, tiled=True)  10.1 us
    all_to_all x1, blocking collectives, block(): lax.all_to_all(scored, 'member', split_axis=0, concat_axis=0, tiled=True)  9.46 us
    pallas_call x1, Pallas kernels, block(): pl.pallas_call(functools.partial(edge_kernel, members=members, own_vars=o...  4.26 us
    pallas_call x1, Pallas kernels, block(): pl.pallas_call(functools.partial(inner_kernel, own_vars=own_vars, n_basis...  3.89 us
    pallas_call x1, Pallas kernels, block(): pl.pallas_call(functools.partial(forward_kernel, circles=circles, rows=ro...  3.02 us
  transfers between devices with their start and end apart: 6, of which 2 were waited for; matrix products, arithmetic and copies ran while one was open for 3% of the time, Pallas kernels for 3%

profile of v1, /device:TPU:88, one launch (start us, length us, event | category | flops | bytes accessed | tf_op | source)
XLA Modules:
  0.0 129.2 jit_solution(2776532822022149939)
XLA Ops:
  0.0 0.0 copy-start
  0.0 2.2 %prepare.1 = (bf16[256,256]{1,0:T(8,128)(2,1)}, bf16[256,256]{1,0:T(8,128)(2,1)}, bf16[64,64]{1,0:T(8,128)(2,1)}, bf16[64,64]{1,0:T(8,128)(2,1)}, f32[4,80,128]{2,1,0:T(8,128)}) custom-call(f32[32,32]{1,0:T(8,128)} %mix_ref.1, f32[8,40,128]{2,1,0:T(8,128)} %t_ref.1), custom_call_target="tpu_custom_call" | custom-call | tf_op jit(solution)/shard_map/prepare/pallas_call | solution.py:340
  2.2 0.9 constant_dynamic-slice_fusion
  3.1 4.7 %collective-permute-start.2 = (f32[1,80,128]{2,1,0:T(8,128)S(1)}, f32[1,80,128]{2,1,0:T(8,128)S(1)}, u32[]{:S(2)}, u32[]{:S(2)}) collective-permute-start(f32[1,80,128]{2,1,0:T(8,128)S(1)} %get-tuple-element.45), channel_id=1, source_target_pairs={{0,384},{128,0},{256,128},{384,256},{1,385},{129,1},{257,129},{385... | collective-permute-start | bytes 122888 | tf_op jit(solution)/shard_map/ppermute | solution.py:358
  7.8 2.7 %collective-permute-start.1 = (f32[1,80,128]{2,1,0:T(8,128)S(1)}, f32[1,80,128]{2,1,0:T(8,128)S(1)}, u32[]{:S(2)}, u32[]{:S(2)}) collective-permute-start(f32[1,80,128]{2,1,0:T(8,128)S(1)} %get-tuple-element.46), channel_id=1, source_target_pairs={{0,256},{128,384},{256,0},{384,128},{1,257},{129,385},{257,1},{385... | collective-permute-start | bytes 122888 | tf_op jit(solution)/shard_map/ppermute | solution.py:358
  10.5 2.8 %collective-permute-start = (f32[1,80,128]{2,1,0:T(8,128)S(1)}, f32[1,80,128]{2,1,0:T(8,128)S(1)}, u32[]{:S(2)}, u32[]{:S(2)}) collective-permute-start(f32[1,80,128]{2,1,0:T(8,128)S(1)} %get-tuple-element.47), channel_id=1, source_target_pairs={{0,128},{128,256},{256,384},{384,0},{1,129},{129,257},{257,385},{3... | collective-permute-start | bytes 122888 | tf_op jit(solution)/shard_map/ppermute | solution.py:358
  13.3 2.3 %send.1 = f32[8,8,40,128]{3,2,1,0:T(8,128)} custom-call(f32[2,32,40,128]{3,2,1,0:T(8,128)} %x_ref.1), custom_call_target="tpu_custom_call" | custom-call | tf_op jit(solution)/shard_map/send/pallas_call | solution.py:325
  15.6 0.0 copy-start.3
  15.6 0.0 copy-start.2
  15.6 0.0 copy-start.1
  15.6 0.0 copy-start.4
  15.6 0.0 copy-start.5
  15.6 10.1 %all-to-all-start = ((f32[8,8,40,128]{3,2,1,0:T(8,128)}), f32[8,8,40,128]{3,2,1,0:T(8,128)S(1)}, u32[]{:S(2)}, u32[]{:S(2)}) async-start(f32[8,8,40,128]{3,2,1,0:T(8,128)} %send.1), calls=%async_computation | async-start | bytes 2621440 | tf_op jit(solution)/shard_map/all_to_all | solution.py:337
  25.7 0.0 copy-done.3
  25.8 0.0 copy-done.2
  25.8 0.1 constant_dynamic-slice_fusion.3
  25.9 0.1 copy.18
  26.0 0.0 copy-done.1
  26.0 0.1 iota_compare_fusion.7
  26.1 0.1 iota_compare_fusion.11
  26.2 0.1 iota_compare_fusion.9
  26.3 0.3 select_add_fusion
  26.6 0.0 copy-done
  26.6 0.0 copy-done.4
  26.6 0.0 copy-done.5
  26.6 0.8 fusion.2
  27.5 0.8 broadcast_multiply_fusion.fac_ref
  28.2 0.7 fusion.4
  29.0 0.7 slice.60
  29.6 0.0 collective-permute-done
  29.6 0.0 collective-permute-done.1
  29.7 0.0 collective-permute-done.2
  29.7 28.1 %all-to-all-done = f32[8,8,40,128]{3,2,1,0:T(8,128)S(1)} async-done(((f32[8,8,40,128]{3,2,1,0:T(8,128)}), f32[8,8,40,128]{3,2,1,0:T(8,128)S(1)}, u32[]{:S(2)}, u32[]{:S(2)}) %all-to-all-start) | async-done | bytes 1310752 | tf_op jit(solution)/shard_map/all_to_all | solution.py:337
  57.8 3.0 %forward.1 = (f32[8,8,1024]{2,1,0:T(8,128)}, f32[8,24,1024]{2,1,0:T(8,128)}, f32[8,8,1024]{2,1,0:T(8,128)}) custom-call(f32[8,320,128]{2,1,0:T(8,128)S(1)} %bitcast.29, bf16[4,256,256]{2,1,0:T(8,128)(2,1)} %constant.89.clone.hi_ref, bf16[4,256,256]{2,1,0:T(8,128)(2,1)} %constant.90.clone.lo_ref), custom_call_target="tpu_custom_call" | custom-call | tf_op jit(solution)/shard_map/forward/pallas_call | solution.py:387
  60.8 1.9 %collective-permute-start.4 = (f32[8,8,1024]{2,1,0:T(8,128)}, f32[8,8,1024]{2,1,0:T(8,128)S(1)}, u32[]{:S(2)}, u32[]{:S(2)}) collective-permute-start(f32[8,8,1024]{2,1,0:T(8,128)} %get-tuple-element.30.top_ref), channel_id=1, source_target_pairs={{8,0},{16,8},{24,16},{32,24},{40,32},{48,40},{56,48},{64,56},{72,6... | collective-permute-start | bytes 786440 | tf_op jit(solution)/shard_map/ppermute | solution.py:398
  62.7 2.4 %collective-permute-start.3 = (f32[8,8,1024]{2,1,0:T(8,128)}, f32[8,8,1024]{2,1,0:T(8,128)S(1)}, u32[]{:S(2)}, u32[]{:S(2)}) collective-permute-start(f32[8,8,1024]{2,1,0:T(8,128)} %get-tuple-element.31.bot_ref), channel_id=1, source_target_pairs={{0,8},{8,16},{16,24},{24,32},{32,40},{40,48},{48,56},{56,64},{64,7... | collective-permute-start | bytes 786440 | tf_op jit(solution)/shard_map/ppermute | solution.py:397
  65.1 3.9 %inner.1 = (f32[3,8,64,128]{3,2,1,0:T(8,128)S(1)}, f32[8,16,1024]{2,1,0:T(8,128)S(1)}) custom-call(f32[8,8,1024]{2,1,0:T(8,128)} %get-tuple-element.30.top_ref, f32[8,24,1024]{2,1,0:T(8,128)} %get-tuple-element.32.mid_ref, f32[8,8,1024]{2,1,0:T(8,128)} %get-tuple-element.31.bot_ref, f32[216,48]{1,0:T(8,128)} %bitcast.32, ...), custom_call_target="tpu_custom_call" | custom-call | tf_op jit(solution)/shard_map/inner/pallas_call | solution.py:399
  69.0 0.0 collective-permute-done.4.dn_ref
  69.1 1.6 %collective-permute-done.3.up_ref = f32[8,8,1024]{2,1,0:T(8,128)S(1)} collective-permute-done((f32[8,8,1024]{2,1,0:T(8,128)}, f32[8,8,1024]{2,1,0:T(8,128)S(1)}, u32[]{:S(2)}, u32[]{:S(2)}) %collective-permute-start.3) | collective-permute-done | bytes 262176 | tf_op jit(solution)/shard_map/ppermute | solution.py:397
  70.6 4.3 %edge.1 = f32[4,8,80,128]{3,2,1,0:T(8,128)} custom-call(f32[8,8,1024]{2,1,0:T(8,128)} %get-tuple-element.30.top_ref, f32[8,8,1024]{2,1,0:T(8,128)} %get-tuple-element.31.bot_ref, f32[8,16,1024]{2,1,0:T(8,128)S(1)} %get-tuple-element.35.near_ref, f32[8,8,1024]{2,1,0:T(8,128)S(1)} %collective-permute-done.3.up_ref, ...), custom_call_target="tpu_custom_call" | custom-call | tf_op jit(solution)/shard_map/edge/pallas_call | solution.py:410
  74.9 41.3 %all_to_all.15 = f32[32,80,128]{2,1,0:T(8,128)S(1)} all-to-all(f32[32,80,128]{2,1,0:T(8,128)} %bitcast.31), channel_id=1, replica_groups=mesh['member'=4,'lat'=16,'lon'=8] {'member','lon'}, dimensions={0} | all-to-all | bytes 2621440 | tf_op jit(solution)/shard_map/all_to_all | solution.py:419
  116.1 2.9 %score.1 = f32[4,80,128]{2,1,0:T(8,128)} custom-call(f32[4,8,80,128]{3,2,1,0:T(8,128)S(1)} %bitcast.30, bf16[256,256]{1,0:T(8,128)(2,1)} %get-tuple-element.38.refs_1_, bf16[256,256]{1,0:T(8,128)(2,1)} %get-tuple-element.39.refs_2_, bf16[64,64]{1,0:T(8,128)(2,1)} %get-tuple-element.40.refs_3_, bf16[64,64]{1,0:T(8,128)(2,1)} %get-tuple-element.41.refs_4_, ...), custom_call_target="tpu_custom_call" | custom-call | tf_op jit(solution)/shard_map/score/pallas_call | solution.py:430
  119.0 9.5 %all_to_all.16.x_ref = f32[4,80,128]{2,1,0:T(8,128)S(1)} all-to-all(f32[4,80,128]{2,1,0:T(8,128)} %score.1), channel_id=1, replica_groups=mesh['member'=4,'lat'=16,'lon'=8] {'member'}, dimensions={0} | all-to-all | bytes 327680 | tf_op jit(solution)/shard_map/all_to_all | solution.py:439
  128.5 0.7 join_rows.1
  (13 shorter events, 0.1 us)
Async XLA Ops:
  0.0 26.6 %copy-start = (f32[9,513]{1,0:T(8,128)S(1)}, f32[9,513]{1,0:T(8,128)}, u32[]{:S(2)}) copy-start(f32[9,513]{1,0:T(8,128)} %param.12) | copy-start | bytes 55408
  3.1 26.6 %collective-permute-start.2 = (f32[1,80,128]{2,1,0:T(8,128)S(1)}, f32[1,80,128]{2,1,0:T(8,128)S(1)}, u32[]{:S(2)}, u32[]{:S(2)}) collective-permute-start(f32[1,80,128]{2,1,0:T(8,128)S(1)} %get-tuple-element.45), channel_id=1, source_target_pairs={{0,384},{128,0},{256,128},{384,256},{1,385},{129,1},{257,129},{385... | collective-permute-start | bytes 122888 | tf_op jit(solution)/shard_map/ppermute | solution.py:358
  7.8 21.9 %collective-permute-start.1 = (f32[1,80,128]{2,1,0:T(8,128)S(1)}, f32[1,80,128]{2,1,0:T(8,128)S(1)}, u32[]{:S(2)}, u32[]{:S(2)}) collective-permute-start(f32[1,80,128]{2,1,0:T(8,128)S(1)} %get-tuple-element.46), channel_id=1, source_target_pairs={{0,256},{128,384},{256,0},{384,128},{1,257},{129,385},{257,1},{385... | collective-permute-start | bytes 122888 | tf_op jit(solution)/shard_map/ppermute | solution.py:358
  10.5 19.1 %collective-permute-start = (f32[1,80,128]{2,1,0:T(8,128)S(1)}, f32[1,80,128]{2,1,0:T(8,128)S(1)}, u32[]{:S(2)}, u32[]{:S(2)}) collective-permute-start(f32[1,80,128]{2,1,0:T(8,128)S(1)} %get-tuple-element.47), channel_id=1, source_target_pairs={{0,128},{128,256},{256,384},{384,0},{1,129},{129,257},{257,385},{3... | collective-permute-start | bytes 122888 | tf_op jit(solution)/shard_map/ppermute | solution.py:358
  15.6 10.2 %copy-start.3 = (s32[40]{0:T(128)S(1)}, s32[40]{0:T(128)}, u32[]{:S(2)}) copy-start(s32[40]{0:T(128)} %param.14) | copy-start | bytes 484
  15.6 10.2 %copy-start.2 = (f32[32,9]{0,1:T(8,128)S(1)}, f32[32,9]{0,1:T(8,128)}, u32[]{:S(2)}) copy-start(f32[32,9]{0,1:T(8,128)} %param.15) | copy-start | bytes 3460
  15.6 10.4 %copy-start.1 = (f32[9,40,5]{1,2,0:T(8,128)S(1)}, f32[9,40,5]{1,2,0:T(8,128)}, u32[]{:S(2)}) copy-start(f32[9,40,5]{1,2,0:T(8,128)} %param.13) | copy-start | bytes 21604
  15.6 11.0 %copy-start.4 = (f32[1024]{0:T(1024)S(1)}, f32[1024]{0:T(1024)}, u32[]{:S(2)}) copy-start(f32[1024]{0:T(1024)} %constant.97) | copy-start | bytes 12292
  15.6 11.0 %copy-start.5 = (s32[1024]{0:T(1024)S(1)}, s32[1024]{0:T(1024)}, u32[]{:S(2)}) copy-start(s32[1024]{0:T(1024)} %constant.91.clone) | copy-start | bytes 12292
  15.6 42.2 %all-to-all-start = ((f32[8,8,40,128]{3,2,1,0:T(8,128)}), f32[8,8,40,128]{3,2,1,0:T(8,128)S(1)}, u32[]{:S(2)}, u32[]{:S(2)}) async-start(f32[8,8,40,128]{3,2,1,0:T(8,128)} %send.1), calls=%async_computation | async-start | bytes 2621440 | tf_op jit(solution)/shard_map/all_to_all | solution.py:337
  60.8 8.2 %collective-permute-start.4 = (f32[8,8,1024]{2,1,0:T(8,128)}, f32[8,8,1024]{2,1,0:T(8,128)S(1)}, u32[]{:S(2)}, u32[]{:S(2)}) collective-permute-start(f32[8,8,1024]{2,1,0:T(8,128)} %get-tuple-element.30.top_ref), channel_id=1, source_target_pairs={{8,0},{16,8},{24,16},{32,24},{40,32},{48,40},{56,48},{64,56},{72,6... | collective-permute-start | bytes 786440 | tf_op jit(solution)/shard_map/ppermute | solution.py:398
  62.7 7.9 %collective-permute-start.3 = (f32[8,8,1024]{2,1,0:T(8,128)}, f32[8,8,1024]{2,1,0:T(8,128)S(1)}, u32[]{:S(2)}, u32[]{:S(2)}) collective-permute-start(f32[8,8,1024]{2,1,0:T(8,128)} %get-tuple-element.31.bot_ref), channel_id=1, source_target_pairs={{0,8},{8,16},{16,24},{24,32},{32,40},{40,48},{48,56},{56,64},{64,7... | collective-permute-start | bytes 786440 | tf_op jit(solution)/shard_map/ppermute | solution.py:397

commit v2 on v1

--- a/solution.py
+++ b/solution.py
@@ -14,25 +14,24 @@
 PTS = 8
 TILE = 128
 LENGTH = PTS * TILE
-ROWPAD = 64
 HALO = 8
+REACH = 5
+GRANT = pltpu.CompilerParams(vmem_limit_bytes=12 << 20)
 S2 = math.sqrt(0.5)
 
 
 def slot_frequencies():
     f1 = np.arange(TILE)
     zero = np.where(f1 <= 64, 8 * f1, 8 * (f1 - 64))
-    four = 8 * (f1 % 64) + 4
-    parts = [zero, four]
+    parts = [zero, 8 * (f1 % 64) + 4]
     for f0 in (1, 2, 3):
         f = 8 * f1 + f0
-        f = np.minimum(f, LENGTH - f)
-        parts += [f, f]
+        parts.append(np.minimum(f, LENGTH - f))
     return np.concatenate(parts).astype(np.int32)
 
 
 def slot_scales():
-    scale = np.full((LENGTH,), 2.0 / LENGTH)
+    scale = np.full((5 * TILE,), 2.0 / LENGTH)
     scale[0] = 1.0 / LENGTH
     scale[64] = 1.0 / LENGTH
     return scale.astype(np.float32)
@@ -80,7 +79,9 @@
 
 def dot3(x, t_hi, t_lo, op):
     hi, lo = split(x)
-    return op(hi, t_hi) + op(lo, t_hi) + op(hi, t_lo)
+    both = op(jnp.concatenate([hi, lo], axis=0), t_hi)
+    size = x.shape[0]
+    return both[:size] + both[size:] + op(hi, t_lo)
 
 
 def analyse(x, hi_ref, lo_ref, store):
@@ -109,18 +110,20 @@
     analyse([x_ref[q] for q in range(PTS)], hi_ref, lo_ref, store)
 
 
-def banded(ext, lhs, fac, count, n_basis):
-    hi, lo = split(ext)
-    z = mm(lhs, jnp.concatenate([hi, hi, lo], axis=0))
-    acc = fac[0:1] * z[:count]
-    for k in range(1, n_basis):
-        acc = acc + fac[k : k + 1] * z[k * count : (k + 1) * count]
+def shifted_sum(ext, coef_ref, c, at, count, lanes):
+    acc = None
+    for e in range(2 * REACH + 1):
+        w = coef_ref[e, c, at : at + count, lanes]
+        if w.shape[1] < ext.shape[1]:
+            w = jnp.concatenate([w, w], axis=1)
+        lead = HALO - REACH + e
+        term = w * ext[lead : lead + count]
+        acc = term if acc is None else acc + term
     return acc
 
 
-def wide_selector(sel_ref):
-    s_hi, s_lo = split(sel_ref[...])
-    return jnp.concatenate([s_hi, s_lo, s_hi], axis=1)
+def coef_lanes(i):
+    return slice(0, 256) if i == 0 else slice(TILE * (i + 1), TILE * (i + 2))
 
 
 def combine(v):
@@ -136,20 +139,18 @@
 
 
 def inner_kernel(
-    top_ref, mid_ref, bot_ref, sel_ref, fac_ref, hi_ref, lo_ref, o_ref, near_ref, y_ref, *, own_vars, n_basis, parts
+    top_ref, mid_ref, bot_ref, coef_ref, hi_ref, lo_ref, o_ref, near_ref, y_ref, *, own_vars, parts
 ):
     circles, count, _ = mid_ref.shape
     near_ref[:, :HALO] = mid_ref[:, :HALO]
     near_ref[:, HALO:] = mid_ref[:, count - HALO :]
-    lhs = wide_selector(sel_ref)
     span = 8 * circles
-    pad = jnp.zeros((8, 256), jnp.float32)
     v = []
     for i in range(4):
         lanes = slice(256 * i, 256 * (i + 1))
         for mc in range(circles):
-            ext = jnp.concatenate([top_ref[mc, :, lanes], mid_ref[mc, :, lanes], bot_ref[mc, :, lanes], pad], axis=0)
-            acc = banded(ext, lhs, fac_ref[mc % own_vars, :, lanes], count, n_basis)
+            ext = jnp.concatenate([top_ref[mc, :, lanes], mid_ref[mc, :, lanes], bot_ref[mc, :, lanes]], axis=0)
+            acc = shifted_sum(ext, coef_ref, mc % own_vars, 0, count, coef_lanes(i))
             for p in range(parts - 1):
                 y_ref[p * span + 8 * mc : p * span + 8 * mc + 8, :] = acc[8 * p : 8 * p + 8]
         v.append(dot3(y_ref[...], hi_ref[i], lo_ref[i], mm_t))
@@ -159,9 +160,8 @@
 
 
 def edge_kernel(
-    top_ref, bot_ref, near_ref, up_ref, dn_ref, in_ref, sel_ref, fac_ref, hi_ref, lo_ref, o_ref, y_ref, *, members, own_vars, n_basis, parts, tail
+    top_ref, bot_ref, near_ref, up_ref, dn_ref, in_ref, coef_ref, hi_ref, lo_ref, o_ref, y_ref, *, members, own_vars, parts, tail
 ):
-    lhs = wide_selector(sel_ref)
     span = 8 * members * own_vars
     main, rest = 8 * own_vars, tail * own_vars
     v = []
@@ -170,14 +170,13 @@
         for m in range(members):
             for c in range(own_vars):
                 mc = m * own_vars + c
-                ext = jnp.concatenate(
-                    [ref[mc, :, lanes] for ref in (top_ref, near_ref, bot_ref, up_ref, dn_ref)], axis=0
-                )
-                acc = banded(ext, lhs, fac_ref[c, :, lanes], 16, n_basis)
-                y_ref[8 * mc : 8 * mc + 8, :] = acc[:8]
+                first = jnp.concatenate([up_ref[mc, :, lanes], top_ref[mc, :, lanes], near_ref[mc, :HALO, lanes]], axis=0)
+                final = jnp.concatenate([near_ref[mc, HALO:, lanes], bot_ref[mc, :, lanes], dn_ref[mc, :, lanes]], axis=0)
+                y_ref[8 * mc : 8 * mc + 8, :] = shifted_sum(first, coef_ref, c, 0, 8, coef_lanes(i))
+                last = shifted_sum(final, coef_ref, c, 8, 8, coef_lanes(i))
                 for p in range(parts):
                     lead = span + (p * members + m) * rest + tail * c
-                    y_ref[lead : lead + tail, :] = acc[8 + tail * p : 8 + tail * (p + 1)]
+                    y_ref[lead : lead + tail, :] = last[tail * p : tail * (p + 1)]
         v.append(dot3(y_ref[...], hi_ref[i], lo_ref[i], mm_t))
     for q, piece in enumerate(combine(v)):
         for p in range(parts):
@@ -333,7 +332,8 @@
             pltpu.SemaphoreType.DMA((n_lon,)),
         ],
         name="send",
-    )(fields)
+        compiler_params=GRANT,
+    )(pltpu.with_memory_space_constraint(fields, pltpu.HBM))
     received = lax.all_to_all(send, "lon", split_axis=0, concat_axis=0, tiled=True)
 
     width = group * (8 + tail)
@@ -347,6 +347,7 @@
             shape((parts, width, tile), f32),
         ),
         name="prepare",
+    compiler_params=GRANT,
     )(mix_weights, target)
     x_at = lax.axis_index("member")
     wanted = jnp.zeros((parts, width, tile), f32)
@@ -359,27 +360,29 @@
         wanted = lax.dynamic_update_slice_in_dim(wanted, got, (x_at - s) % n_member, 0)
 
     hi_np, lo_np = dft_tables()
-    hi, lo = jnp.asarray(hi_np), jnp.asarray(lo_np)
-
-    local_start = band_start - lax.axis_index("lat") * rows
-    read = local_start[:, None] + jnp.arange(band_len, dtype=jnp.int32)[None, :]
-    pos = jnp.where(read < 0, rows + HALO + read, jnp.where(read < rows, read, read + HALO))
-    cols = jnp.arange(ROWPAD, dtype=jnp.int32)
-    sel = jnp.zeros((n_basis, rows, ROWPAD), f32)
+    hi, lo = in_vmem(jnp.asarray(hi_np), jnp.asarray(lo_np))
+
+    first_row = lax.axis_index("lat") * rows
+    offset = band_start - first_row - jnp.arange(rows, dtype=jnp.int32) + REACH
+    step = jnp.arange(2 * REACH + 1, dtype=jnp.int32)[:, None]
+    spread = jnp.zeros((n_basis, 2 * REACH + 1, rows), f32)
     for j in range(band_len):
-        sel = sel + jnp.where(pos[None, :, j, None] == cols, band_weights[:, :, j, None], 0.0)
-    inner_sel = sel[:, 8 : rows - 8, : rows + 8].reshape(n_basis * (rows - 16), rows + 8)
-    edge_sel = jnp.concatenate([sel[:, :8], sel[:, rows - 8 :]], axis=1)
-    edge_sel = jnp.concatenate([edge_sel[:, :, :16], edge_sel[:, :, rows - 16 : rows + 16]], axis=2)
-    edge_sel = edge_sel.reshape(n_basis * 16, 48)
-
+        spread = spread + jnp.where(offset[None, :] + j == step, band_weights[:, None, :, j], 0.0)
     freq = jnp.asarray(slot_frequencies())
     pick = (jnp.arange(spectra.shape[1], dtype=jnp.int32)[:, None] == freq[None, :]).astype(f32)
     spec = jnp.dot(spectra, pick, precision=lax.Precision.HIGHEST) * slot_scales()[None, :]
     depth = lax.dynamic_slice_in_dim(depth_weights, lax.axis_index("lon") * own_vars, own_vars, 0)
-    factor = depth[:, :, None] * spec[None]
-    received, krons, wanted, inner_sel, edge_sel, factor = lax.optimization_barrier(
-        (received, krons, wanted, inner_sel, edge_sel, factor)
+    basis = spread[:, :, None, :] * depth.T[:, None, :, None]
+
+    def coefficients(part):
+        flat = part.reshape(n_basis, -1)
+        out = lax.dot_general(flat, spec, (((0,), (0,)), ((), ())), precision=lax.Precision.HIGHEST)
+        return out.reshape(*part.shape[1:], spec.shape[1])
+
+    inner_coef = coefficients(basis[:, :, :, HALO : rows - HALO])
+    edge_coef = coefficients(jnp.concatenate([basis[:, :, :, :HALO], basis[:, :, :, rows - HALO :]], axis=3))
+    received, krons, wanted, inner_coef, edge_coef = lax.optimization_barrier(
+        (received, krons, wanted, inner_coef, edge_coef)
     )
 
     up = [(i, i + 1) for i in range(n_lat - 1)]
@@ -387,35 +390,40 @@
     top, mid, bot = pl.pallas_call(
         functools.partial(forward_kernel, circles=circles, rows=rows),
         out_shape=(
-            shape((circles, HALO, LENGTH), f32),
-            shape((circles, rows - 2 * HALO, LENGTH), f32),
-            shape((circles, HALO, LENGTH), f32),
+            pltpu.VMEM((circles, HALO, LENGTH), f32),
+            pltpu.VMEM((circles, rows - 2 * HALO, LENGTH), f32),
+            pltpu.VMEM((circles, HALO, LENGTH), f32),
         ),
         in_specs=[vmem] * 3,
+        out_specs=(vmem, vmem, vmem),
         name="forward",
+        compiler_params=GRANT,
     )(*in_vmem(received.reshape(n_lon, circles * rows, tile)), hi, lo)
     before = lax.ppermute(bot, "lat", up)
     after = lax.ppermute(top, "lat", down)
     inner, near = pl.pallas_call(
-        functools.partial(inner_kernel, own_vars=own_vars, n_basis=n_basis, parts=parts),
+        functools.partial(inner_kernel, own_vars=own_vars, parts=parts),
         out_shape=(
             pltpu.VMEM((parts - 1, n_lon, 8 * circles, tile), f32),
             pltpu.VMEM((circles, 2 * HALO, LENGTH), f32),
         ),
-        in_specs=[vmem] * 7,
+        in_specs=[vmem] * 6,
         out_specs=(vmem, vmem),
         scratch_shapes=[pltpu.VMEM((8 * (parts - 1) * circles, 256), f32)],
         name="inner",
-    )(top, mid, bot, inner_sel, factor, hi, lo)
+    compiler_params=GRANT,
+    )(*in_vmem(top, mid, bot, inner_coef), hi, lo)
     smooth = pl.pallas_call(
         functools.partial(
-            edge_kernel, members=members, own_vars=own_vars, n_basis=n_basis, parts=parts, tail=tail
+            edge_kernel, members=members, own_vars=own_vars, parts=parts, tail=tail
         ),
-        out_shape=shape((parts, n_lon, circles * (8 + tail), tile), f32),
-        in_specs=[vmem] * 10,
+        out_shape=pltpu.VMEM((parts, n_lon, circles * (8 + tail), tile), f32),
+        in_specs=[vmem] * 9,
+        out_specs=vmem,
         scratch_shapes=[pltpu.VMEM((circles * (8 + parts * tail), 256), f32)],
         name="edge",
-    )(top, bot, *in_vmem(near, before, after, inner), edge_sel, factor, hi, lo)
+        compiler_params=GRANT,
+    )(*in_vmem(top, bot, near, before, after, inner, edge_coef), hi, lo)
     moved = lax.all_to_all(
         smooth.reshape(parts * n_lon, *smooth.shape[2:]),
         ("member", "lon"),
@@ -431,17 +439,20 @@
         functools.partial(
             score_kernel, total=total, main=variables * 8, parts=parts, earlier=0, sizes=sizes
         ),
-        out_shape=shape((parts, width, tile), f32),
+        out_shape=pltpu.VMEM((parts, width, tile), f32),
         in_specs=[vmem] * 6,
+        out_specs=vmem,
         scratch_shapes=[pltpu.VMEM((total, height, tile), f32)],
         name="score",
-    )(*in_vmem(moved), *krons, *in_vmem(wanted))
+        compiler_params=GRANT,
+    )(*in_vmem(moved, *krons, wanted))
     back = lax.all_to_all(scored, "member", split_axis=0, concat_axis=0, tiled=True)
     return pl.pallas_call(
         functools.partial(join_rows_kernel, parts=parts, tail=tail),
         out_shape=shape(target.shape, f32),
         in_specs=[vmem],
         name="join_rows",
+        compiler_params=GRANT,
     )(*in_vmem(back))
 
 

time: 130 us -> 124 us (0.954)
  the two profiles are of different devices: /device:TPU:88 before, /device:TPU:24 now
where the time goes in v2:
time: 124 us; the launch traced here: 123 us
  blocking collectives  47.7 us (38%)
  waiting for transfers between devices  26.8 us (22%)
  starting transfers between devices  24.9 us (20%)
  Pallas kernels  9.64 us (8%)
  local copies, waits for them, and re-layouts  7.64 us (6%)
  matrix products  5.81 us (5%)
    all_to_all x1, blocking collectives, block(): lax.all_to_all(smooth.reshape(parts * n_lon, *smooth.shape[2:]), ('member...  38.4 us
    all_to_all x1, waiting for transfers between devices, block(): lax.all_to_all(send, 'lon', split_axis=0, concat_axis=0, tiled=True)  23 us
    all_to_all x1, starting transfers between devices, block(): lax.all_to_all(send, 'lon', split_axis=0, concat_axis=0, tiled=True)  10.5 us
    ppermute x3, starting transfers between devices, block(): got = lax.ppermute(out, 'member', ring)  10.2 us
    all_to_all x1, blocking collectives, block(): lax.all_to_all(scored, 'member', split_axis=0, concat_axis=0, tiled=True)  9.26 us
    dot_general x2, matrix products, coefficients(): lax.dot_general(flat, spec, (((0,), (0,)), ((), ())), precision=lax.Preci...  5.25 us
    ppermute x1, waiting for transfers between devices, block(): before = lax.ppermute(bot, 'lat', up)  3.7 us
    unnamed x35, local copies, waits for them, and re-layouts  2.76 us
  transfers between devices with their start and end apart: 6, of which 2 were waited for; matrix products, arithmetic and copies ran while one was open for 8% of the time, Pallas kernels for 1%

profile of v2, /device:TPU:24, one launch (start us, length us, event | category | flops | bytes accessed | tf_op | source)
XLA Modules:
  0.0 123.2 jit_solution(17353247704386148330)
XLA Ops:
  0.0 0.0 copy-start
  0.0 0.9 copy-done.5
  0.9 0.7 copy-done.10
  1.6 0.6 prepare.1
  2.2 0.0 copy-start.8
  2.3 0.7 constant_dynamic-slice_fusion
  2.9 0.0 copy-done.6
  2.9 0.0 copy-done.8
  2.9 4.7 %collective-permute-start.2 = (f32[1,80,128]{2,1,0:T(8,128)S(1)}, f32[1,80,128]{2,1,0:T(8,128)}, u32[]{:S(2)}, u32[]{:S(2)}) collective-permute-start(f32[1,80,128]{2,1,0:T(8,128)S(1)} %get-tuple-element.45), channel_id=1, source_target_pairs={{0,384},{128,0},{256,128},{384,256},{1,385},{129,1},{257,129},{385... | collective-permute-start | bytes 122888 | tf_op jit(solution)/shard_map/ppermute | solution.py:359
  7.6 2.7 %collective-permute-start.1 = (f32[1,80,128]{2,1,0:T(8,128)S(1)}, f32[1,80,128]{2,1,0:T(8,128)}, u32[]{:S(2)}, u32[]{:S(2)}) collective-permute-start(f32[1,80,128]{2,1,0:T(8,128)S(1)} %get-tuple-element.46), channel_id=1, source_target_pairs={{0,256},{128,384},{256,0},{384,128},{1,257},{129,385},{257,1},{385... | collective-permute-start | bytes 122888 | tf_op jit(solution)/shard_map/ppermute | solution.py:359
  10.3 2.8 %collective-permute-start = (f32[1,80,128]{2,1,0:T(8,128)}, f32[1,80,128]{2,1,0:T(8,128)}, u32[]{:S(2)}, u32[]{:S(2)}) collective-permute-start(f32[1,80,128]{2,1,0:T(8,128)} %get-tuple-element.47), channel_id=1, source_target_pairs={{0,128},{128,256},{256,384},{384,0},{1,129},{129,257},{257,385},{3... | collective-permute-start | bytes 122888 | tf_op jit(solution)/shard_map/ppermute | solution.py:359
  13.1 2.3 %send.1 = f32[8,8,40,128]{3,2,1,0:T(8,128)} custom-call(f32[2,32,40,128]{3,2,1,0:T(8,128)} %x_ref.1), custom_call_target="tpu_custom_call" | custom-call | tf_op jit(solution)/shard_map/send/pallas_call | solution.py:324
  15.4 0.0 copy-start.14
  15.4 0.0 copy-start.12
  15.4 0.0 copy-start.13
  15.4 10.5 %all-to-all-start = ((f32[8,8,40,128]{3,2,1,0:T(8,128)}), f32[8,8,40,128]{3,2,1,0:T(8,128)}, u32[]{:S(2)}, u32[]{:S(2)}) async-start(f32[8,8,40,128]{3,2,1,0:T(8,128)} %send.1), calls=%async_computation | async-start | bytes 2621440 | tf_op jit(solution)/shard_map/all_to_all | solution.py:337
  25.9 0.0 copy-done.14
  25.9 0.0 copy-done.12
  26.0 0.0 copy-done.13
  26.0 0.1 dynamic-slice_bitcast_fusion
  26.1 0.1 broadcast_multiply_fusion
  26.3 0.2 slice.32
  26.4 0.0 copy-start.15
  26.4 0.0 copy-start.16
  26.4 0.2 reshape.44
  26.6 0.2 dot_general.18
  26.8 0.2 fusion.8
  27.0 0.2 pad_maximum_fusion
  27.2 1.1 copy.24
  28.2 0.0 copy-done
  28.2 0.0 copy-done.15
  28.2 0.0 copy-done.16
  28.2 0.6 fusion.2
  28.8 0.0 copy-start.11
  28.8 2.5 %fusion.6.coef_ref = f32[11,4,24,640]{3,2,1,0:T(8,128)S(1)} fusion(f32[640,9,1,1]{0,1,3,2:T(8,128)S(1)} %fusion.2, f32[11,4,24,9]{2,1,0,3:T(4,128)S(1)} %dot_general.18), kind=kOutput, calls=%fused_computation.7 | convolution fusion | flops 72990720 | bytes 2764416 | tf_op jit(solution)/shard_map/dot_general | solution.py:379
  31.3 0.0 copy-done.11
  31.3 0.0 copy-start.2
  31.3 2.8 %fusion.4.coef_ref = f32[11,4,16,640]{3,2,1,0:T(8,128)} fusion(f32[640,9,1,1]{0,1,3,2:T(8,128)S(1)} %fusion.2, f32[9,11,4,16]{0,3,2,1:T(8,128)S(1)} %copy-done.11), kind=kOutput, calls=%fused_computation.5 | convolution fusion | flops 48660480 | bytes 1850624 | tf_op jit(solution)/shard_map/dot_general | solution.py:379
  34.1 0.0 collective-permute-done
  34.1 0.8 constant_dynamic-update-slice_fusion.2
  34.9 0.0 collective-permute-done.1
  34.9 0.8 constant_dynamic-update-slice_fusion.1
  35.7 0.0 collective-permute-done.2
  35.7 0.8 constant_dynamic-update-slice_fusion.refs_5_
  36.5 23.0 %all-to-all-done = f32[8,8,40,128]{3,2,1,0:T(8,128)} async-done(((f32[8,8,40,128]{3,2,1,0:T(8,128)}), f32[8,8,40,128]{3,2,1,0:T(8,128)}, u32[]{:S(2)}, u32[]{:S(2)}) %all-to-all-start) | async-done | bytes 1310752 | tf_op jit(solution)/shard_map/all_to_all | solution.py:337
  59.5 0.0 copy-done.2
  59.5 1.0 copy-done.3
  60.6 2.1 %forward.1 = (f32[8,8,1024]{2,1,0:T(8,128)S(1)}, f32[8,24,1024]{2,1,0:T(8,128)S(1)}, f32[8,8,1024]{2,1,0:T(8,128)S(1)}) custom-call(f32[8,320,128]{2,1,0:T(8,128)} %bitcast.13.x_ref, bf16[4,256,256]{2,1,0:T(8,128)(2,1)S(1)} %copy-done.3, bf16[4,256,256]{2,1,0:T(8,128)(2,1)S(1)} %copy-done.2), custom_call_target="tpu_custom_call" | custom-call | tf_op jit(solution)/shard_map/forward/pallas_call | solution.py:390
  62.7 2.0 %collective-permute-start.4 = (f32[8,8,1024]{2,1,0:T(8,128)S(1)}, f32[8,8,1024]{2,1,0:T(8,128)S(1)}, u32[]{:S(2)}, u32[]{:S(2)}) collective-permute-start(f32[8,8,1024]{2,1,0:T(8,128)S(1)} %get-tuple-element.29.top_ref), channel_id=1, source_target_pairs={{8,0},{16,8},{24,16},{32,24},{40,32},{48,40},{56,48},{64,56},{72,6... | collective-permute-start | bytes 786440 | tf_op jit(solution)/shard_map/ppermute | solution.py:403
  64.7 2.3 %collective-permute-start.3 = (f32[8,8,1024]{2,1,0:T(8,128)S(1)}, f32[8,8,1024]{2,1,0:T(8,128)S(1)}, u32[]{:S(2)}, u32[]{:S(2)}) collective-permute-start(f32[8,8,1024]{2,1,0:T(8,128)S(1)} %get-tuple-element.30.bot_ref), channel_id=1, source_target_pairs={{0,8},{8,16},{16,24},{24,32},{32,40},{40,48},{48,56},{56,64},{64,7... | collective-permute-start | bytes 786440 | tf_op jit(solution)/shard_map/ppermute | solution.py:402
  67.0 0.0 copy-done.4
  67.0 0.0 copy-start.1
  67.0 1.6 %inner.1 = (f32[3,8,64,128]{3,2,1,0:T(8,128)S(1)}, f32[8,16,1024]{2,1,0:T(8,128)S(1)}) custom-call(f32[8,8,1024]{2,1,0:T(8,128)S(1)} %get-tuple-element.29.top_ref, f32[8,24,1024]{2,1,0:T(8,128)S(1)} %get-tuple-element.31.mid_ref, f32[8,8,1024]{2,1,0:T(8,128)S(1)} %get-tuple-element.30.bot_ref, f32[11,4,24,640]{3,2,1,0:T(8,128)S(1)} %fusion.6.coef_ref, ...), custom_call_target="tpu_custom_call" | custom-call | tf_op jit(solution)/shard_map/inner/pallas_call | solution.py:404
  68.6 0.0 collective-permute-done.4.dn_ref
  68.6 3.7 %collective-permute-done.3.up_ref = f32[8,8,1024]{2,1,0:T(8,128)S(1)} collective-permute-done((f32[8,8,1024]{2,1,0:T(8,128)S(1)}, f32[8,8,1024]{2,1,0:T(8,128)S(1)}, u32[]{:S(2)}, u32[]{:S(2)}) %collective-permute-start.3) | collective-permute-done | bytes 262176 | tf_op jit(solution)/shard_map/ppermute | solution.py:402
  72.4 0.0 copy-done.1
  72.4 1.2 edge.1
  73.6 0.0 copy-start.7
  73.6 0.0 copy-start.9
  73.6 38.4 %all_to_all.15 = f32[32,80,128]{2,1,0:T(8,128)S(1)} all-to-all(f32[32,80,128]{2,1,0:T(8,128)S(1)} %bitcast.34), channel_id=1, replica_groups=mesh['member'=4,'lat'=16,'lon'=8] {'member','lon'}, dimensions={0} | all-to-all | bytes 2621440 | tf_op jit(solution)/shard_map/all_to_all | solution.py:427
  112.0 0.0 copy-done.7
  112.0 1.2 score.1
  113.2 9.3 %all_to_all.16.x_ref = f32[4,80,128]{2,1,0:T(8,128)S(1)} all-to-all(f32[4,80,128]{2,1,0:T(8,128)S(1)} %score.1), channel_id=1, replica_groups=mesh['member'=4,'lat'=16,'lon'=8] {'member'}, dimensions={0} | all-to-all | bytes 327680 | tf_op jit(solution)/shard_map/all_to_all | solution.py:449
  122.5 0.7 join_rows.1
  (17 shorter events, 0.1 us)
Async XLA Ops:
  0.0 28.2 %copy-start = (f32[9,513]{1,0:T(8,128)S(1)}, f32[9,513]{1,0:T(8,128)}, u32[]{:S(2)}) copy-start(f32[9,513]{1,0:T(8,128)} %param.12) | copy-start | bytes 55408
  0.0 0.9 copy-start.5
  0.9 0.7 copy-start.10
  2.2 0.7 copy-start.6
  2.2 0.7 copy-start.8
  2.9 32.8 %collective-permute-start.2 = (f32[1,80,128]{2,1,0:T(8,128)S(1)}, f32[1,80,128]{2,1,0:T(8,128)}, u32[]{:S(2)}, u32[]{:S(2)}) collective-permute-start(f32[1,80,128]{2,1,0:T(8,128)S(1)} %get-tuple-element.45), channel_id=1, source_target_pairs={{0,384},{128,0},{256,128},{384,256},{1,385},{129,1},{257,129},{385... | collective-permute-start | bytes 122888 | tf_op jit(solution)/shard_map/ppermute | solution.py:359
  7.6 27.3 %collective-permute-start.1 = (f32[1,80,128]{2,1,0:T(8,128)S(1)}, f32[1,80,128]{2,1,0:T(8,128)}, u32[]{:S(2)}, u32[]{:S(2)}) collective-permute-start(f32[1,80,128]{2,1,0:T(8,128)S(1)} %get-tuple-element.46), channel_id=1, source_target_pairs={{0,256},{128,384},{256,0},{384,128},{1,257},{129,385},{257,1},{385... | collective-permute-start | bytes 122888 | tf_op jit(solution)/shard_map/ppermute | solution.py:359
  10.3 23.8 %collective-permute-start = (f32[1,80,128]{2,1,0:T(8,128)}, f32[1,80,128]{2,1,0:T(8,128)}, u32[]{:S(2)}, u32[]{:S(2)}) collective-permute-start(f32[1,80,128]{2,1,0:T(8,128)} %get-tuple-element.47), channel_id=1, source_target_pairs={{0,128},{128,256},{256,384},{384,0},{1,129},{129,257},{257,385},{3... | collective-permute-start | bytes 122888 | tf_op jit(solution)/shard_map/ppermute | solution.py:359
  15.4 10.5 %copy-start.14 = (s32[40]{0:T(128)S(1)}, s32[40]{0:T(128)}, u32[]{:S(2)}) copy-start(s32[40]{0:T(128)} %param.14) | copy-start | bytes 484
  15.4 10.5 %copy-start.12 = (f32[9,40,5]{1,2,0:T(8,128)S(1)}, f32[9,40,5]{1,2,0:T(8,128)}, u32[]{:S(2)}) copy-start(f32[9,40,5]{1,2,0:T(8,128)} %param.13) | copy-start | bytes 21604
  15.4 10.6 %copy-start.13 = (f32[32,9]{0,1:T(8,128)S(1)}, f32[32,9]{0,1:T(8,128)}, u32[]{:S(2)}) copy-start(f32[32,9]{0,1:T(8,128)} %param.15) | copy-start | bytes 3460
  15.4 44.1 %all-to-all-start = ((f32[8,8,40,128]{3,2,1,0:T(8,128)}), f32[8,8,40,128]{3,2,1,0:T(8,128)}, u32[]{:S(2)}, u32[]{:S(2)}) async-start(f32[8,8,40,128]{3,2,1,0:T(8,128)} %send.1), calls=%async_computation | async-start | bytes 2621440 | tf_op jit(solution)/shard_map/all_to_all | solution.py:337
  26.4 1.8 %copy-start.15 = (f32[640]{0:T(1024)S(1)}, f32[640]{0:T(1024)}, u32[]{:S(2)}) copy-start(f32[640]{0:T(1024)} %constant.105) | copy-start | bytes 7684
  26.4 1.8 %copy-start.16 = (s32[640]{0:T(1024)S(1)}, s32[640]{0:T(1024)}, u32[]{:S(2)}) copy-start(s32[640]{0:T(1024)} %constant.99.clone) | copy-start | bytes 7684
  28.8 2.5 %copy-start.11 = (f32[9,11,4,16]{0,3,2,1:T(8,128)S(1)}, f32[9,11,4,16]{0,3,2,1:T(8,128)}, u32[]{:S(2)}) copy-start(f32[9,11,4,16]{0,3,2,1:T(8,128)} %copy.24) | copy-start | bytes 76036
  31.3 28.2 %copy-start.2 = (bf16[4,256,256]{2,1,0:T(8,128)(2,1)S(1)}, bf16[4,256,256]{2,1,0:T(8,128)(2,1)}, u32[]{:S(2)}) copy-start(bf16[4,256,256]{2,1,0:T(8,128)(2,1)} %constant.98.clone.lo_ref) | copy-start | bytes 1572868
  59.5 1.0 copy-start.3
  60.5 6.5 %copy-start.4 = (bf16[4,256,256]{2,1,0:T(8,128)(2,1)S(1)}, bf16[4,256,256]{2,1,0:T(8,128)(2,1)}, u32[]{:S(2)}) copy-start(bf16[4,256,256]{2,1,0:T(8,128)(2,1)} %constant.97.clone.hi_ref) | copy-start | bytes 1572868
  62.7 6.0 %collective-permute-start.4 = (f32[8,8,1024]{2,1,0:T(8,128)S(1)}, f32[8,8,1024]{2,1,0:T(8,128)S(1)}, u32[]{:S(2)}, u32[]{:S(2)}) collective-permute-start(f32[8,8,1024]{2,1,0:T(8,128)S(1)} %get-tuple-element.29.top_ref), channel_id=1, source_target_pairs={{8,0},{16,8},{24,16},{32,24},{40,32},{48,40},{56,48},{64,56},{72,6... | collective-permute-start | bytes 786440 | tf_op jit(solution)/shard_map/ppermute | solution.py:403
  64.7 7.7 %collective-permute-start.3 = (f32[8,8,1024]{2,1,0:T(8,128)S(1)}, f32[8,8,1024]{2,1,0:T(8,128)S(1)}, u32[]{:S(2)}, u32[]{:S(2)}) collective-permute-start(f32[8,8,1024]{2,1,0:T(8,128)S(1)} %get-tuple-element.30.bot_ref), channel_id=1, source_target_pairs={{0,8},{8,16},{16,24},{24,32},{32,40},{40,48},{48,56},{56,64},{64,7... | collective-permute-start | bytes 786440 | tf_op jit(solution)/shard_map/ppermute | solution.py:402
  67.0 5.3 %copy-start.1 = (f32[11,4,16,640]{3,2,1,0:T(8,128)S(1)}, f32[11,4,16,640]{3,2,1,0:T(8,128)}, u32[]{:S(2)}) copy-start(f32[11,4,16,640]{3,2,1,0:T(8,128)} %fusion.4.coef_ref) | copy-start | bytes 5406724
  73.6 38.5 %copy-start.7 = (bf16[256,256]{1,0:T(8,128)(2,1)S(1)}, bf16[256,256]{1,0:T(8,128)(2,1)}, u32[]{:S(2)}) copy-start(bf16[256,256]{1,0:T(8,128)(2,1)} %copy-done.6) | copy-start | bytes 393220
  73.6 38.4 %copy-start.9 = (bf16[256,256]{1,0:T(8,128)(2,1)S(1)}, bf16[256,256]{1,0:T(8,128)(2,1)}, u32[]{:S(2)}) copy-start(bf16[256,256]{1,0:T(8,128)(2,1)} %copy-done.8) | copy-start | bytes 393220

commit v3 on v2

--- a/solution.py
+++ b/solution.py
@@ -57,10 +57,22 @@
         tabs[f0, TILE:, :TILE] = s
         tabs[f0, :TILE, TILE:] = -s
         tabs[f0, TILE:, TILE:] = c
-    full = tabs.astype(np.float32)
-    hi = full.astype(ml_dtypes.bfloat16)
-    lo = (tabs - hi.astype(np.float64)).astype(ml_dtypes.bfloat16)
-    return hi, lo
+    pairs = np.zeros((4, 2, TILE, TILE))
+    pairs[0, 0], pairs[0, 1] = tabs[0, :TILE, :TILE], tabs[0, TILE:, TILE:]
+    pairs[1:, 0], pairs[1:, 1] = tabs[1:, :TILE, :TILE], tabs[1:, TILE:, :TILE]
+    hi = pairs.astype(ml_dtypes.bfloat16)
+    lo = (pairs - hi.astype(np.float64)).astype(ml_dtypes.bfloat16)
+    return np.stack([hi, lo])
+
+
+def whole_table(t_ref, level, i):
+    a, b = t_ref[level, i, 0], t_ref[level, i, 1]
+    if i == 0:
+        none = jnp.zeros_like(a)
+        upper, lower = (a, none), (none, b)
+    else:
+        upper, lower = (a, -b), (b, a)
+    return jnp.concatenate([jnp.concatenate(upper, axis=1), jnp.concatenate(lower, axis=1)], axis=0)
 
 
 def split(x):
@@ -84,7 +96,7 @@
     return both[:size] + both[size:] + op(hi, t_lo)
 
 
-def analyse(x, hi_ref, lo_ref, store):
+def analyse(x, t_ref, store):
     a = [x[q] + x[q + 4] for q in range(4)]
     b = [x[q] - x[q + 4] for q in range(4)]
     e, g = a[0] + a[2], a[1] + a[3]
@@ -96,10 +108,10 @@
         (b[0] - m, b[2] - p),
     ]
     for i, pair in enumerate(pairs):
-        store(i, dot3(jnp.concatenate(pair, axis=1), hi_ref[i], lo_ref[i], mm))
-
-
-def forward_kernel(x_ref, hi_ref, lo_ref, top_ref, mid_ref, bot_ref, *, circles, rows):
+        store(i, dot3(jnp.concatenate(pair, axis=1), whole_table(t_ref, 0, i), whole_table(t_ref, 1, i), mm))
+
+
+def forward_kernel(x_ref, t_ref, top_ref, mid_ref, bot_ref, *, circles, rows):
     def store(i, z):
         lanes = slice(256 * i, 256 * (i + 1))
         z = z.reshape(circles, rows, 256)
@@ -107,7 +119,7 @@
         mid_ref[:, :, lanes] = z[:, HALO : rows - HALO]
         bot_ref[:, :, lanes] = z[:, rows - HALO :]
 
-    analyse([x_ref[q] for q in range(PTS)], hi_ref, lo_ref, store)
+    analyse([x_ref[q] for q in range(PTS)], t_ref, store)
 
 
 def shifted_sum(ext, coef_ref, c, at, count, lanes):
@@ -139,7 +151,7 @@
 
 
 def inner_kernel(
-    top_ref, mid_ref, bot_ref, coef_ref, hi_ref, lo_ref, o_ref, near_ref, y_ref, *, own_vars, parts
+    top_ref, mid_ref, bot_ref, coef_ref, t_ref, o_ref, near_ref, y_ref, *, own_vars, parts
 ):
     circles, count, _ = mid_ref.shape
     near_ref[:, :HALO] = mid_ref[:, :HALO]
@@ -153,14 +165,14 @@
             acc = shifted_sum(ext, coef_ref, mc % own_vars, 0, count, coef_lanes(i))
             for p in range(parts - 1):
                 y_ref[p * span + 8 * mc : p * span + 8 * mc + 8, :] = acc[8 * p : 8 * p + 8]
-        v.append(dot3(y_ref[...], hi_ref[i], lo_ref[i], mm_t))
+        v.append(dot3(y_ref[...], whole_table(t_ref, 0, i), whole_table(t_ref, 1, i), mm_t))
     for q, piece in enumerate(combine(v)):
         for p in range(parts - 1):
             o_ref[p, q] = piece[p * span : (p + 1) * span]
 
 
 def edge_kernel(
-    top_ref, bot_ref, near_ref, up_ref, dn_ref, in_ref, coef_ref, hi_ref, lo_ref, o_ref, y_ref, *, members, own_vars, parts, tail
+    top_ref, bot_ref, near_ref, up_ref, dn_ref, in_ref, coef_ref, t_ref, o_ref, y_ref, *, members, own_vars, parts, tail
 ):
     span = 8 * members * own_vars
     main, rest = 8 * own_vars, tail * own_vars
@@ -177,7 +189,7 @@
                 for p in range(parts):
                     lead = span + (p * members + m) * rest + tail * c
                     y_ref[lead : lead + tail, :] = last[tail * p : tail * (p + 1)]
-        v.append(dot3(y_ref[...], hi_ref[i], lo_ref[i], mm_t))
+        v.append(dot3(y_ref[...], whole_table(t_ref, 0, i), whole_table(t_ref, 1, i), mm_t))
     for q, piece in enumerate(combine(v)):
         for p in range(parts):
             for m in range(members):
@@ -359,8 +371,7 @@
         got = lax.ppermute(out, "member", ring)
         wanted = lax.dynamic_update_slice_in_dim(wanted, got, (x_at - s) % n_member, 0)
 
-    hi_np, lo_np = dft_tables()
-    hi, lo = in_vmem(jnp.asarray(hi_np), jnp.asarray(lo_np))
+    (table,) = in_vmem(jnp.asarray(dft_tables()))
 
     first_row = lax.axis_index("lat") * rows
     offset = band_start - first_row - jnp.arange(rows, dtype=jnp.int32) + REACH
@@ -394,11 +405,11 @@
             pltpu.VMEM((circles, rows - 2 * HALO, LENGTH), f32),
             pltpu.VMEM((circles, HALO, LENGTH), f32),
         ),
-        in_specs=[vmem] * 3,
+        in_specs=[vmem] * 2,
         out_specs=(vmem, vmem, vmem),
         name="forward",
         compiler_params=GRANT,
-    )(*in_vmem(received.reshape(n_lon, circles * rows, tile)), hi, lo)
+    )(*in_vmem(received.reshape(n_lon, circles * rows, tile)), table)
     before = lax.ppermute(bot, "lat", up)
     after = lax.ppermute(top, "lat", down)
     inner, near = pl.pallas_call(
@@ -407,23 +418,23 @@
             pltpu.VMEM((parts - 1, n_lon, 8 * circles, tile), f32),
             pltpu.VMEM((circles, 2 * HALO, LENGTH), f32),
         ),
-        in_specs=[vmem] * 6,
+        in_specs=[vmem] * 5,
         out_specs=(vmem, vmem),
         scratch_shapes=[pltpu.VMEM((8 * (parts - 1) * circles, 256), f32)],
         name="inner",
     compiler_params=GRANT,
-    )(*in_vmem(top, mid, bot, inner_coef), hi, lo)
+    )(*in_vmem(top, mid, bot, inner_coef), table)
     smooth = pl.pallas_call(
         functools.partial(
             edge_kernel, members=members, own_vars=own_vars, parts=parts, tail=tail
         ),
         out_shape=pltpu.VMEM((parts, n_lon, circles * (8 + tail), tile), f32),
-        in_specs=[vmem] * 9,
+        in_specs=[vmem] * 8,
         out_specs=vmem,
         scratch_shapes=[pltpu.VMEM((circles * (8 + parts * tail), 256), f32)],
         name="edge",
         compiler_params=GRANT,
-    )(*in_vmem(top, bot, near, before, after, inner, edge_coef), hi, lo)
+    )(*in_vmem(top, bot, near, before, after, inner, edge_coef), table)
     moved = lax.all_to_all(
         smooth.reshape(parts * n_lon, *smooth.shape[2:]),
         ("member", "lon"),

time: 124 us -> 123 us (level)
    unnamed x35 -> x31, local copies, waits for them, and re-layouts: 2.76 us -> 1.71 us
where the time goes in v3:
time: 123 us; the launch traced here: 122 us
  blocking collectives  47.7 us (39%)
  waiting for transfers between devices  26.8 us (22%)
  starting transfers between devices  24.9 us (20%)
  Pallas kernels  9.57 us (8%)
  local copies, waits for them, and re-layouts  6.6 us (5%)
  matrix products  5.8 us (5%)
    all_to_all x1, blocking collectives, block(): lax.all_to_all(smooth.reshape(parts * n_lon, *smooth.shape[2:]), ('member...  38.4 us
    all_to_all x1, waiting for transfers between devices, block(): lax.all_to_all(send, 'lon', split_axis=0, concat_axis=0, tiled=True)  23 us
    all_to_all x1, starting transfers between devices, block(): lax.all_to_all(send, 'lon', split_axis=0, concat_axis=0, tiled=True)  10.5 us
    ppermute x3, starting transfers between devices, block(): got = lax.ppermute(out, 'member', ring)  10.2 us
    all_to_all x1, blocking collectives, block(): lax.all_to_all(scored, 'member', split_axis=0, concat_axis=0, tiled=True)  9.25 us
    dot_general x2, matrix products, coefficients(): lax.dot_general(flat, spec, (((0,), (0,)), ((), ())), precision=lax.Preci...  5.24 us
    ppermute x1, waiting for transfers between devices, block(): before = lax.ppermute(bot, 'lat', up)  3.73 us
  transfers between devices with their start and end apart: 6, of which 2 were waited for; matrix products, arithmetic and copies ran while one was open for 8% of the time, Pallas kernels for 1%

profile of v3, /device:TPU:24, one launch (start us, length us, event | category | flops | bytes accessed | tf_op | source)
XLA Modules:
  0.0 122.1 jit_solution(6676803413511063470)
XLA Ops:
  0.0 0.0 copy-start
  0.0 0.0 copy-start.3
  0.0 0.9 copy-done.3
  0.9 0.7 copy-done.8
  1.6 0.6 prepare.1
  2.2 0.0 copy-start.6
  2.3 0.7 constant_dynamic-slice_fusion
  2.9 0.0 copy-done.4
  2.9 0.0 copy-done.6
  2.9 4.7 %collective-permute-start.2 = (f32[1,80,128]{2,1,0:T(8,128)S(1)}, f32[1,80,128]{2,1,0:T(8,128)}, u32[]{:S(2)}, u32[]{:S(2)}) collective-permute-start(f32[1,80,128]{2,1,0:T(8,128)S(1)} %get-tuple-element.45), channel_id=1, source_target_pairs={{0,384},{128,0},{256,128},{384,256},{1,385},{129,1},{257,129},{385... | collective-permute-start | bytes 122888 | tf_op jit(solution)/shard_map/ppermute | solution.py:371
  7.6 2.7 %collective-permute-start.1 = (f32[1,80,128]{2,1,0:T(8,128)S(1)}, f32[1,80,128]{2,1,0:T(8,128)}, u32[]{:S(2)}, u32[]{:S(2)}) collective-permute-start(f32[1,80,128]{2,1,0:T(8,128)S(1)} %get-tuple-element.46), channel_id=1, source_target_pairs={{0,256},{128,384},{256,0},{384,128},{1,257},{129,385},{257,1},{385... | collective-permute-start | bytes 122888 | tf_op jit(solution)/shard_map/ppermute | solution.py:371
  10.3 2.8 %collective-permute-start = (f32[1,80,128]{2,1,0:T(8,128)}, f32[1,80,128]{2,1,0:T(8,128)}, u32[]{:S(2)}, u32[]{:S(2)}) collective-permute-start(f32[1,80,128]{2,1,0:T(8,128)} %get-tuple-element.47), channel_id=1, source_target_pairs={{0,128},{128,256},{256,384},{384,0},{1,129},{129,257},{257,385},{3... | collective-permute-start | bytes 122888 | tf_op jit(solution)/shard_map/ppermute | solution.py:371
  13.1 2.3 %send.1 = f32[8,8,40,128]{3,2,1,0:T(8,128)} custom-call(f32[2,32,40,128]{3,2,1,0:T(8,128)} %x_ref.1), custom_call_target="tpu_custom_call" | custom-call | tf_op jit(solution)/shard_map/send/pallas_call | solution.py:336
  15.4 0.0 copy-start.12
  15.4 0.0 copy-start.10
  15.4 0.0 copy-start.11
  15.4 10.5 %all-to-all-start = ((f32[8,8,40,128]{3,2,1,0:T(8,128)}), f32[8,8,40,128]{3,2,1,0:T(8,128)}, u32[]{:S(2)}, u32[]{:S(2)}) async-start(f32[8,8,40,128]{3,2,1,0:T(8,128)} %send.1), calls=%async_computation | async-start | bytes 2621440 | tf_op jit(solution)/shard_map/all_to_all | solution.py:349
  25.9 0.0 copy-done.12
  25.9 0.0 copy-done.10
  26.0 0.0 copy-done.11
  26.0 0.1 dynamic-slice_bitcast_fusion
  26.1 0.1 broadcast_multiply_fusion
  26.2 0.2 slice.32
  26.4 0.0 copy-start.13
  26.4 0.0 copy-start.14
  26.4 0.2 reshape.44
  26.6 0.2 dot_general.18
  26.8 0.2 fusion.8
  27.0 0.2 pad_maximum_fusion
  27.2 1.1 copy.23
  28.2 0.0 copy-done
  28.2 0.0 copy-done.13
  28.2 0.0 copy-done.14
  28.2 0.6 fusion.2
  28.8 0.0 copy-start.9
  28.8 2.5 %fusion.6.coef_ref = f32[11,4,24,640]{3,2,1,0:T(8,128)S(1)} fusion(f32[640,9,1,1]{0,1,3,2:T(8,128)S(1)} %fusion.2, f32[11,4,24,9]{2,1,0,3:T(4,128)S(1)} %dot_general.18), kind=kOutput, calls=%fused_computation.7 | convolution fusion | flops 72990720 | bytes 2764416 | tf_op jit(solution)/shard_map/dot_general | solution.py:390
  31.3 0.0 copy-done.9
  31.3 0.0 copy-start.2
  31.3 2.8 %fusion.4.coef_ref = f32[11,4,16,640]{3,2,1,0:T(8,128)} fusion(f32[640,9,1,1]{0,1,3,2:T(8,128)S(1)} %fusion.2, f32[9,11,4,16]{0,3,2,1:T(8,128)S(1)} %copy-done.9), kind=kOutput, calls=%fused_computation.5 | convolution fusion | flops 48660480 | bytes 1850624 | tf_op jit(solution)/shard_map/dot_general | solution.py:390
  34.1 0.0 collective-permute-done
  34.1 0.8 constant_dynamic-update-slice_fusion.2
  34.9 0.0 collective-permute-done.1
  34.9 0.8 constant_dynamic-update-slice_fusion.1
  35.7 0.0 collective-permute-done.2
  35.7 0.8 constant_dynamic-update-slice_fusion.refs_5_
  36.5 23.0 %all-to-all-done = f32[8,8,40,128]{3,2,1,0:T(8,128)} async-done(((f32[8,8,40,128]{3,2,1,0:T(8,128)}), f32[8,8,40,128]{3,2,1,0:T(8,128)}, u32[]{:S(2)}, u32[]{:S(2)}) %all-to-all-start) | async-done | bytes 1310752 | tf_op jit(solution)/shard_map/all_to_all | solution.py:349
  59.5 0.0 copy-done.2
  59.5 2.1 %forward.1 = (f32[8,8,1024]{2,1,0:T(8,128)S(1)}, f32[8,24,1024]{2,1,0:T(8,128)S(1)}, f32[8,8,1024]{2,1,0:T(8,128)S(1)}) custom-call(f32[8,320,128]{2,1,0:T(8,128)} %bitcast.13.x_ref, bf16[2,4,2,128,128]{4,3,2,1,0:T(8,128)(2,1)S(1)} %copy-done.2), custom_call_target="tpu_custom_call" | custom-call | tf_op jit(solution)/shard_map/forward/pallas_call | solution.py:401
  61.6 2.0 %collective-permute-start.4 = (f32[8,8,1024]{2,1,0:T(8,128)S(1)}, f32[8,8,1024]{2,1,0:T(8,128)S(1)}, u32[]{:S(2)}, u32[]{:S(2)}) collective-permute-start(f32[8,8,1024]{2,1,0:T(8,128)S(1)} %get-tuple-element.29.top_ref), channel_id=1, source_target_pairs={{8,0},{16,8},{24,16},{32,24},{40,32},{48,40},{56,48},{64,56},{72,6... | collective-permute-start | bytes 786440 | tf_op jit(solution)/shard_map/ppermute | solution.py:414
  63.5 2.3 %collective-permute-start.3 = (f32[8,8,1024]{2,1,0:T(8,128)S(1)}, f32[8,8,1024]{2,1,0:T(8,128)S(1)}, u32[]{:S(2)}, u32[]{:S(2)}) collective-permute-start(f32[8,8,1024]{2,1,0:T(8,128)S(1)} %get-tuple-element.30.bot_ref), channel_id=1, source_target_pairs={{0,8},{8,16},{16,24},{24,32},{32,40},{40,48},{48,56},{56,64},{64,7... | collective-permute-start | bytes 786440 | tf_op jit(solution)/shard_map/ppermute | solution.py:413
  65.9 0.0 copy-start.1
  65.9 1.6 %inner.1 = (f32[3,8,64,128]{3,2,1,0:T(8,128)S(1)}, f32[8,16,1024]{2,1,0:T(8,128)S(1)}) custom-call(f32[8,8,1024]{2,1,0:T(8,128)S(1)} %get-tuple-element.29.top_ref, f32[8,24,1024]{2,1,0:T(8,128)S(1)} %get-tuple-element.31.mid_ref, f32[8,8,1024]{2,1,0:T(8,128)S(1)} %get-tuple-element.30.bot_ref, f32[11,4,24,640]{3,2,1,0:T(8,128)S(1)} %fusion.6.coef_ref, ...), custom_call_target="tpu_custom_call" | custom-call | tf_op jit(solution)/shard_map/inner/pallas_call | solution.py:415
  67.5 0.0 collective-permute-done.4.dn_ref
  67.5 3.7 %collective-permute-done.3.up_ref = f32[8,8,1024]{2,1,0:T(8,128)S(1)} collective-permute-done((f32[8,8,1024]{2,1,0:T(8,128)S(1)}, f32[8,8,1024]{2,1,0:T(8,128)S(1)}, u32[]{:S(2)}, u32[]{:S(2)}) %collective-permute-start.3) | collective-permute-done | bytes 262176 | tf_op jit(solution)/shard_map/ppermute | solution.py:413
  71.2 0.0 copy-done.1
  71.2 1.2 edge.1
  72.5 0.0 copy-start.5
  72.5 0.0 copy-start.7
  72.5 38.4 %all_to_all.15 = f32[32,80,128]{2,1,0:T(8,128)S(1)} all-to-all(f32[32,80,128]{2,1,0:T(8,128)S(1)} %bitcast.34), channel_id=1, replica_groups=mesh['member'=4,'lat'=16,'lon'=8] {'member','lon'}, dimensions={0} | all-to-all | bytes 2621440 | tf_op jit(solution)/shard_map/all_to_all | solution.py:438
  110.9 0.0 copy-done.5
  110.9 0.0 copy-done.7
  110.9 1.2 score.1
  112.1 9.3 %all_to_all.16.x_ref = f32[4,80,128]{2,1,0:T(8,128)S(1)} all-to-all(f32[4,80,128]{2,1,0:T(8,128)S(1)} %score.1), channel_id=1, replica_groups=mesh['member'=4,'lat'=16,'lon'=8] {'member'}, dimensions={0} | all-to-all | bytes 327680 | tf_op jit(solution)/shard_map/all_to_all | solution.py:460
  121.4 0.7 join_rows.1
  (13 shorter events, 0.1 us)
Async XLA Ops:
  0.0 28.2 %copy-start = (f32[9,513]{1,0:T(8,128)S(1)}, f32[9,513]{1,0:T(8,128)}, u32[]{:S(2)}) copy-start(f32[9,513]{1,0:T(8,128)} %param.11) | copy-start | bytes 55408
  0.0 0.9 copy-start.3
  0.9 0.7 copy-start.8
  2.2 0.7 copy-start.4
  2.2 0.7 copy-start.6
  2.9 32.7 %collective-permute-start.2 = (f32[1,80,128]{2,1,0:T(8,128)S(1)}, f32[1,80,128]{2,1,0:T(8,128)}, u32[]{:S(2)}, u32[]{:S(2)}) collective-permute-start(f32[1,80,128]{2,1,0:T(8,128)S(1)} %get-tuple-element.45), channel_id=1, source_target_pairs={{0,384},{128,0},{256,128},{384,256},{1,385},{129,1},{257,129},{385... | collective-permute-start | bytes 122888 | tf_op jit(solution)/shard_map/ppermute | solution.py:371
  7.6 27.3 %collective-permute-start.1 = (f32[1,80,128]{2,1,0:T(8,128)S(1)}, f32[1,80,128]{2,1,0:T(8,128)}, u32[]{:S(2)}, u32[]{:S(2)}) collective-permute-start(f32[1,80,128]{2,1,0:T(8,128)S(1)} %get-tuple-element.46), channel_id=1, source_target_pairs={{0,256},{128,384},{256,0},{384,128},{1,257},{129,385},{257,1},{385... | collective-permute-start | bytes 122888 | tf_op jit(solution)/shard_map/ppermute | solution.py:371
  10.3 23.8 %collective-permute-start = (f32[1,80,128]{2,1,0:T(8,128)}, f32[1,80,128]{2,1,0:T(8,128)}, u32[]{:S(2)}, u32[]{:S(2)}) collective-permute-start(f32[1,80,128]{2,1,0:T(8,128)} %get-tuple-element.47), channel_id=1, source_target_pairs={{0,128},{128,256},{256,384},{384,0},{1,129},{129,257},{257,385},{3... | collective-permute-start | bytes 122888 | tf_op jit(solution)/shard_map/ppermute | solution.py:371
  15.4 10.5 %copy-start.12 = (s32[40]{0:T(128)S(1)}, s32[40]{0:T(128)}, u32[]{:S(2)}) copy-start(s32[40]{0:T(128)} %param.13) | copy-start | bytes 484
  15.4 10.5 %copy-start.10 = (f32[9,40,5]{1,2,0:T(8,128)S(1)}, f32[9,40,5]{1,2,0:T(8,128)}, u32[]{:S(2)}) copy-start(f32[9,40,5]{1,2,0:T(8,128)} %param.12) | copy-start | bytes 21604
  15.4 10.6 %copy-start.11 = (f32[32,9]{0,1:T(8,128)S(1)}, f32[32,9]{0,1:T(8,128)}, u32[]{:S(2)}) copy-start(f32[32,9]{0,1:T(8,128)} %param.14) | copy-start | bytes 3460
  15.4 44.1 %all-to-all-start = ((f32[8,8,40,128]{3,2,1,0:T(8,128)}), f32[8,8,40,128]{3,2,1,0:T(8,128)}, u32[]{:S(2)}, u32[]{:S(2)}) async-start(f32[8,8,40,128]{3,2,1,0:T(8,128)} %send.1), calls=%async_computation | async-start | bytes 2621440 | tf_op jit(solution)/shard_map/all_to_all | solution.py:349
  26.4 1.8 %copy-start.13 = (f32[640]{0:T(1024)S(1)}, f32[640]{0:T(1024)}, u32[]{:S(2)}) copy-start(f32[640]{0:T(1024)} %constant.102) | copy-start | bytes 7684
  26.4 1.8 %copy-start.14 = (s32[640]{0:T(1024)S(1)}, s32[640]{0:T(1024)}, u32[]{:S(2)}) copy-start(s32[640]{0:T(1024)} %constant.96.clone) | copy-start | bytes 7684
  28.8 2.5 %copy-start.9 = (f32[9,11,4,16]{0,3,2,1:T(8,128)S(1)}, f32[9,11,4,16]{0,3,2,1:T(8,128)}, u32[]{:S(2)}) copy-start(f32[9,11,4,16]{0,3,2,1:T(8,128)} %copy.23) | copy-start | bytes 76036
  31.3 28.2 %copy-start.2 = (bf16[2,4,2,128,128]{4,3,2,1,0:T(8,128)(2,1)S(1)}, bf16[2,4,2,128,128]{4,3,2,1,0:T(8,128)(2,1)}, u32[]{:S(2)}) copy-start(bf16[2,4,2,128,128]{4,3,2,1,0:T(8,128)(2,1)} %constant.95.clone.t_ref) | copy-start | bytes 1572868
  61.6 5.9 %collective-permute-start.4 = (f32[8,8,1024]{2,1,0:T(8,128)S(1)}, f32[8,8,1024]{2,1,0:T(8,128)S(1)}, u32[]{:S(2)}, u32[]{:S(2)}) collective-permute-start(f32[8,8,1024]{2,1,0:T(8,128)S(1)} %get-tuple-element.29.top_ref), channel_id=1, source_target_pairs={{8,0},{16,8},{24,16},{32,24},{40,32},{48,40},{56,48},{64,56},{72,6... | collective-permute-start | bytes 786440 | tf_op jit(solution)/shard_map/ppermute | solution.py:414
  63.5 7.7 %collective-permute-start.3 = (f32[8,8,1024]{2,1,0:T(8,128)S(1)}, f32[8,8,1024]{2,1,0:T(8,128)S(1)}, u32[]{:S(2)}, u32[]{:S(2)}) collective-permute-start(f32[8,8,1024]{2,1,0:T(8,128)S(1)} %get-tuple-element.30.bot_ref), channel_id=1, source_target_pairs={{0,8},{8,16},{16,24},{24,32},{32,40},{40,48},{48,56},{56,64},{64,7... | collective-permute-start | bytes 786440 | tf_op jit(solution)/shard_map/ppermute | solution.py:413
  65.9 5.3 %copy-start.1 = (f32[11,4,16,640]{3,2,1,0:T(8,128)S(1)}, f32[11,4,16,640]{3,2,1,0:T(8,128)}, u32[]{:S(2)}) copy-start(f32[11,4,16,640]{3,2,1,0:T(8,128)} %fusion.4.coef_ref) | copy-start | bytes 5406724
  72.5 38.5 %copy-start.5 = (bf16[256,256]{1,0:T(8,128)(2,1)S(1)}, bf16[256,256]{1,0:T(8,128)(2,1)}, u32[]{:S(2)}) copy-start(bf16[256,256]{1,0:T(8,128)(2,1)} %copy-done.4) | copy-start | bytes 393220
  72.5 38.4 %copy-start.7 = (bf16[256,256]{1,0:T(8,128)(2,1)S(1)}, bf16[256,256]{1,0:T(8,128)(2,1)}, u32[]{:S(2)}) copy-start(bf16[256,256]{1,0:T(8,128)(2,1)} %copy-done.6) | copy-start | bytes 393220
